TPU v7x, 512 devices: a whole 4x4x16 slice. The times are simulated.
512 devices in a mesh: section: 2 (over x_hi), expert: 32 (over z, core), tensor: 8 (over x_lo, y).
Axes of the slice: x: 4 (x_hi: 2, x_lo: 2; x = x_hi * 2 + x_lo), y: 4, z: 16, core: 2. Of those that a mesh axis runs over, the one named last changes fastest.
Arguments:
- tokens: bfloat16 [8192, 2880], P(('section', 'expert'), 'tensor'), may hold values from -6 to 6
- expert_ids: int32 [8192, 4], P(('section', 'expert')), may hold values from 0 to 63, as said below
- gates: float32 [8192, 4], P(('section', 'expert')), may hold values from 0.05 to 0.5
- remap: int32 [64], replicated, may hold values from 0 to 63, as said below
- gate_up: bfloat16 [64, 2, 1440, 2880], P(('section', 'expert'), None, 'tensor'), may hold values from -0.109375 to 0.109375
- down: bfloat16 [64, 1440, 2880], P(('section', 'expert'), None, 'tensor'), may hold values from -0.15625 to 0.15625
- norm_gain: float32 [2880], replicated, may hold values from 0.25 to 1.75
- w_query: bfloat16 [2880, 2048], P(('section', 'expert'), 'tensor'), may hold values from -2 to 2
- w_key: bfloat16 [2880, 512], P(('section', 'expert'), 'tensor'), may hold values from -2 to 2
- w_value: bfloat16 [2880, 512], P(('section', 'expert'), 'tensor'), may hold values from -0.109375 to 0.109375
- w_out: bfloat16 [2048, 2880], P('tensor', ('section', 'expert')), may hold values from -0.125 to 0.125
Outputs:
- stream: bfloat16 [8192, 2880], P(('section', 'expert'), 'tensor')
- attended: bfloat16 [8192, 2880], P(('section', 'expert'), 'tensor')
Inputs may be any that keep to these rules, and one draw needn't show every extreme that they name: `remap`: every expert maps to itself, except the 4 experts of one aligned group of 4 (a failed host), which map to 4 different surviving experts. `expert_ids`: each row names 4 different experts, and their images under remap differ too. In every aligned block of 128 rows, after the remap, 4 surviving experts receive exactly 16 picks each, every other surviving expert exactly 8, the experts of the failed host none.
All inputs are finite; a program needn't handle non-finite values.
Results may differ from a plain program's by a relative error of at most 0.033.
Values may be sent and summed in bfloat16 or wider, within the bound.
No kernel may reach another device: no remote copies, remote signals or barrier semaphores. Data moves between devices by JAX's collectives and lax.ppermute only.
A program may use at most 64 MiB of HBM per device.

v0:
```python
import math

import jax
import jax.numpy as jnp
from jax import lax
from jax.sharding import PartitionSpec as P

D = 2880
HD = 64


epsilon = 1e-05


def rotate_pairs(values, positions):
    half_size = values.shape[-1] // 2
    freq = jnp.exp(
        -math.log(150000.0) * jnp.arange(half_size, dtype=jnp.float32) * 2.0 / values.shape[-1]
    )
    angle = positions.astype(jnp.float32)[:, None] * freq[None, :]
    cosine = jnp.cos(angle)[:, None, :]
    sine = jnp.sin(angle)[:, None, :]
    first_half = values[..., :half_size]
    second_half = values[..., half_size:]
    return jnp.concatenate(
        [first_half * cosine - second_half * sine, second_half * cosine + first_half * sine],
        axis=-1,
    )


def on_device(
    tokens, expert_ids, gates, remap, gate_up, down, norm_gain, w_query, w_key, w_value, w_out
):
    token_rows = tokens.shape[0]
    slice_width = tokens.shape[1]
    topk_count = expert_ids.shape[1]
    groups = lax.axis_size(("section", "expert"))
    capacity = 2 * token_rows * topk_count // groups
    physical = remap[expert_ids].reshape(-1)
    pick_count = physical.shape[0]
    pick_token = jnp.arange(pick_count, dtype=jnp.int32) // topk_count
    one_hot = (physical[:, None] == jnp.arange(groups, dtype=jnp.int32)[None, :]).astype(jnp.int32)
    pick_rank = jnp.sum((jnp.cumsum(one_hot, axis=0) - 1) * one_hot, axis=1)
    slot_index = physical * capacity + pick_rank
    slot_hits = slot_index[:, None] == jnp.arange(groups * capacity, dtype=jnp.int32)[None, :]
    slot_token = jnp.sum(jnp.where(slot_hits, pick_token[:, None], 0), axis=0)
    slot_used = jnp.any(slot_hits, axis=0)
    local_hidden = gate_up.shape[2]
    local_expert = gate_up[0].reshape(2 * local_hidden, gate_up.shape[3])
    whole_tokens = lax.all_gather(tokens, "tensor", axis=1, tiled=True)
    outgoing = jnp.where(
        slot_used[:, None], whole_tokens[slot_token], jnp.zeros((), jnp.bfloat16)
    ).reshape(groups, capacity, -1)
    arrived = lax.all_to_all(
        outgoing, ("section", "expert"), split_axis=0, concat_axis=0, tiled=True
    )
    source_count = arrived.shape[0]
    rows_in = arrived.reshape(-1, arrived.shape[2])
    projected = lax.dot_general(
        rows_in, local_expert, (((1,), (1,)), ((), ())), preferred_element_type=jnp.float32
    )
    hidden = (jax.nn.silu(projected[:, :local_hidden]) * projected[:, local_hidden:]).astype(
        jnp.bfloat16
    )
    all_hidden = lax.all_gather(hidden, "tensor", axis=1, tiled=True)
    result = jnp.dot(all_hidden, down[0], preferred_element_type=jnp.float32).astype(jnp.bfloat16)
    result = result.reshape(source_count, -1, result.shape[1])
    returned = lax.all_to_all(
        result, ("section", "expert"), split_axis=0, concat_axis=0, tiled=True
    )
    back_rows = returned.reshape(groups * capacity, -1)[slot_index]
    mixture = jnp.sum(
        back_rows.astype(jnp.float32).reshape(token_rows, topk_count, -1) * gates[:, :, None],
        axis=1,
    )
    stream = (tokens.astype(jnp.float32) + mixture).astype(jnp.bfloat16)
    stream_wide = stream.astype(jnp.float32)
    squares = lax.psum(jnp.sum(stream_wide * stream_wide, axis=1), "tensor")
    gain_part = lax.dynamic_slice_in_dim(
        norm_gain, lax.axis_index("tensor") * slice_width, slice_width
    )
    normed_part = (
        stream_wide * lax.rsqrt(squares / D + epsilon)[:, None] * gain_part[None, :]
    ).astype(jnp.bfloat16)
    normed = lax.all_gather(normed_part, "tensor", axis=1, tiled=True)
    query_width = w_query.shape[1]
    kv_width = w_key.shape[1]
    pieces = (
        lax.all_gather(w_query, ("section", "expert"), axis=0, tiled=True),
        lax.all_gather(w_key, ("section", "expert"), axis=0, tiled=True),
        lax.all_gather(w_value, ("section", "expert"), axis=0, tiled=True),
    )
    query_raw, key_raw, value_raw = tuple(
        (jnp.dot(normed, piece, preferred_element_type=jnp.float32) for piece in pieces)
    )
    positions = lax.axis_index("expert") * token_rows + jnp.arange(token_rows, dtype=jnp.int32)
    query_heads = query_width // HD
    kv_heads = kv_width // HD
    group_size = query_heads // kv_heads
    queries = rotate_pairs(query_raw.reshape(token_rows, query_heads, HD), positions).astype(
        jnp.bfloat16
    )
    keys = (
        rotate_pairs(key_raw.reshape(token_rows, kv_heads, HD), positions)
        .astype(jnp.bfloat16)
        .reshape(token_rows, kv_width)
    )
    values = value_raw.astype(jnp.bfloat16)
    grouped = queries.reshape(token_rows, kv_heads, group_size, HD)
    pieces = (
        lax.all_gather(keys, "expert", axis=0, tiled=True),
        lax.all_gather(values, "expert", axis=0, tiled=True),
    )
    running_max = jnp.full((kv_heads, group_size, token_rows), -1e30, jnp.float32)
    key_piece = pieces[0].reshape(-1, kv_heads, HD)
    value_piece = pieces[1].reshape(-1, kv_heads, HD)
    key_count = key_piece.shape[0]
    scores = jnp.einsum(
        "tkgd,nkd->kgtn", grouped, key_piece, preferred_element_type=jnp.float32
    ) / math.sqrt(HD)
    key_positions = jnp.arange(key_count, dtype=jnp.int32)
    allowed = key_positions[None, :] <= positions[:, None]
    scores = jnp.where(allowed, scores, -1e30)
    new_max = jnp.maximum(running_max, jnp.max(scores, axis=-1))
    weights = jnp.where(allowed, jnp.exp(scores - new_max[..., None]), 0.0)
    new_sum = jnp.sum(weights, axis=-1)
    weights_low = weights.astype(jnp.bfloat16)
    new_acc = jnp.einsum(
        "kgtn,nkd->kgtd", weights_low, value_piece, preferred_element_type=jnp.float32
    )
    heads = (
        (new_acc / new_sum[..., None])
        .transpose(2, 0, 1, 3)
        .reshape(token_rows, query_width)
        .astype(jnp.bfloat16)
    )
    partial_out = jnp.dot(
        heads,
        lax.all_gather(w_out, ("section", "expert"), axis=1, tiled=True),
        preferred_element_type=jnp.float32,
    )
    attended = lax.psum_scatter(
        partial_out.astype(jnp.bfloat16), "tensor", scatter_dimension=1, tiled=True
    )
    return (stream, attended)


def solution(mesh):
    return jax.shard_map(
        on_device,
        mesh=mesh,
        in_specs=(
            P(("section", "expert"), "tensor"),
            P(("section", "expert"), None),
            P(("section", "expert"), None),
            P(),
            P(("section", "expert"), None, "tensor", None),
            P(("section", "expert"), None, "tensor"),
            P(),
            P(("section", "expert"), "tensor"),
            P(("section", "expert"), "tensor"),
            P(("section", "expert"), "tensor"),
            P("tensor", ("section", "expert")),
        ),
        out_specs=(P(("section", "expert"), "tensor"), P(("section", "expert"), "tensor")),
        check_vma=False,
    )
```

profile of v0, /device:TPU:1, one launch (start us, length us, event | category | flops | bytes accessed | tf_op | source)
XLA Modules:
  0.0 849.4 jit_solution(9896610226944616474)
XLA Ops:
  7.2 0.8 compare_select_fusion.2
  8.2 3.3 gather_fusion
  11.6 1.2 reduce-window.6
  13.2 0.4 fusion.7
  13.9 24.8 %all_gather.27 = bf16[128,2880]{0,1:T(8,128)(2,1)S(1)} all-gather(bf16[128,360]{0,1:T(8,128)(2,1)S(1)} %copy-done.5), channel_id=1, replica_groups=mesh['section'=2,'expert'=32,'tensor'=8] {'tensor'}, dimensions={1}, use_global_device_ids=true | all-gather | bytes 829440 | tf_op jit(solution)/shard_map/all_gather | solution.py:50
  38.7 0.4 copy.57
  39.1 6.6 gather_fusion.1
  45.7 5.9 broadcast_select_fusion
  51.6 24.8 %all-to-all-start = ((bf16[64,16,2880]{2,1,0:T(8,128)(2,1)}), bf16[64,16,2880]{2,1,0:T(8,128)(2,1)}, u32[]{:S(2)}, u32[]{:S(2)}) async-start(bf16[64,16,2880]{2,1,0:T(8,128)(2,1)} %broadcast_select_fusion), calls=%async_computation | async-start | bytes 12058624 | tf_op jit(solution)/shard_map/all_to_all | solution.py:54
  76.5 1.8 copy.58
  78.3 2.3 reshape_squeeze.3
  80.7 261.0 %all-to-all-done = bf16[64,16,2880]{2,1,0:T(8,128)(2,1)} async-done(((bf16[64,16,2880]{2,1,0:T(8,128)(2,1)}), bf16[64,16,2880]{2,1,0:T(8,128)(2,1)}, u32[]{:S(2)}, u32[]{:S(2)}) %all-to-all-start) | async-done | bytes 5898272 | tf_op jit(solution)/shard_map/all_to_all | solution.py:54
  341.6 5.8 fusion.47
  347.5 1.0 fusion.19
  348.5 0.7 all-gather.11.cloned.1.call-update
  349.3 0.7 all-gather.13.cloned.1.call-update
  350.0 41.6 %all-gather.9.cloned.1.call-done = bf16[8,180,1024]{2,1,0:T(8,128)(2,1)} async-done(((bf16[1,180,1024]{2,1,0:T(8,128)(2,1)}), bf16[8,180,1024]{2,1,0:T(8,128)(2,1)}) %all-gather.9.cloned.1.call-update) | async-done | bytes 2949136 | tf_op jit(solution)/shard_map/all_gather | solution.py:65
  391.5 4.3 reshape.315
  395.9 3.2 convolution_convert_fusion.1
  399.1 1.2 copy.59
  400.3 18.4 %all-to-all-start.1 = ((bf16[64,16,360]{2,1,0:T(8,128)(2,1)}), bf16[64,16,360]{2,1,0:T(8,128)(2,1)S(1)}, u32[]{:S(2)}, u32[]{:S(2)}) async-start(bf16[64,16,360]{2,1,0:T(8,128)(2,1)} %bitcast.9), calls=%async_computation.1 | async-start | bytes 1572864 | tf_op jit(solution)/shard_map/all_to_all | solution.py:68
  419.0 107.5 %all-gather.1 = bf16[64,45,64]{2,1,0:T(8,128)(2,1)S(1)} all-gather(bf16[1,45,64]{2,1,0:T(8,128)(2,1)S(1)} %bitcast.105), channel_id=1, replica_groups=mesh['section'=2,'expert'=32,'tensor'=8] {'section','expert'}, dimensions={0}, use_global_device_ids=true | all-gather | bytes 374400 | tf_op jit(solution)/shard_map/all_gather | solution.py:90
  526.5 1.1 reshape.326
  527.6 73.9 %all-gather.3 = bf16[64,45,64]{2,1,0:T(8,128)(2,1)S(1)} all-gather(bf16[1,45,64]{2,1,0:T(8,128)(2,1)S(1)} %bitcast.106), channel_id=1, replica_groups=mesh['section'=2,'expert'=32,'tensor'=8] {'section','expert'}, dimensions={0}, use_global_device_ids=true | all-gather | bytes 374400 | tf_op jit(solution)/shard_map/all_gather | solution.py:91
  601.5 1.1 reshape.327
  602.6 0.8 dynamic_slice.3
  603.5 0.8 multiply_cosine_fusion
  604.2 1.1 iota_compare_fusion
  605.4 3.4 reshape.319
  608.8 74.8 %all-gather.13.cloned.1.call-done = bf16[64,45,256]{2,1,0:T(8,128)(2,1)} async-done(((bf16[1,45,256]{2,1,0:T(8,128)(2,1)}), bf16[64,45,256]{2,1,0:T(8,128)(2,1)}) %all-gather.13.cloned.1.call-update) | async-done | bytes 1474576 | tf_op jit(solution)/shard_map/all_gather | solution.py:139
  683.6 2.4 reshape.323
  686.0 2.6 gather_fusion.2
  688.6 1.2 reshape.281
  689.8 0.5 multiply_reduce_fusion
  690.5 15.1 %psum.7 = f32[128]{0:T(128)S(1)} all-reduce(f32[128]{0:T(128)S(1)} %get-tuple-element.8), channel_id=1, replica_groups=mesh['section'=2,'expert'=32,'tensor'=8] {'tensor'}, use_global_device_ids=true, to_apply=%region_7.8 | all-reduce | flops 128 | bytes 1024 | tf_op jit(solution)/shard_map/psum | solution.py:78
  705.8 24.6 %all_gather.29 = bf16[128,2880]{0,1:T(8,128)(2,1)S(1)} all-gather(bf16[128,360]{0,1:T(8,128)(2,1)S(1)} %copy.61), channel_id=1, replica_groups=mesh['section'=2,'expert'=32,'tensor'=8] {'tensor'}, dimensions={1}, use_global_device_ids=true | all-gather | bytes 829440 | tf_op jit(solution)/shard_map/all_gather | solution.py:85
  730.4 1.5 convolution_bitcast_fusion
  731.9 0.7 fusion.38
  732.7 39.0 %all_gather.31 = bf16[4096,64]{0,1:T(8,128)(2,1)S(1)} all-gather(bf16[128,64]{0,1:T(8,128)(2,1)S(1)} %pad_maximum_fusion), channel_id=1, replica_groups=mesh['section'=2,'expert'=32,'tensor'=8] {'expert'}, dimensions={0}, use_global_device_ids=true | all-gather | bytes 540672 | tf_op jit(solution)/shard_map/all_gather | solution.py:111
  771.7 0.7 fusion.48
  772.5 1.3 fusion
  773.8 0.4 convolution_convert_fusion.2
  774.2 28.5 %all_gather.34 = bf16[4096,64]{0,1:T(8,128)(2,1)S(1)} all-gather(bf16[128,64]{0,1:T(8,128)(2,1)S(1)} %convolution_convert_fusion.2), channel_id=1, replica_groups=mesh['section'=2,'expert'=32,'tensor'=8] {'expert'}, dimensions={0}, use_global_device_ids=true | all-gather | bytes 540672 | tf_op jit(solution)/shard_map/all_gather | solution.py:112
  802.7 2.1 fusion.1
  804.8 1.8 fusion.12
  806.6 1.4 convolution_convert_fusion
  808.1 0.8 copy.66
  808.8 34.0 %reduce-scatter.5.cloned.1.call-done = bf16[128,360]{0,1:T(8,128)(2,1)} async-done(((bf16[128,2880]{0,1:T(8,128)(2,1)}), bf16[128,360]{0,1:T(8,128)(2,1)}) %reduce-scatter.5.cloned.1.call-update) | async-done | bytes 92176
  (61 shorter events, 1.9 us)
Async XLA Ops:
  7.2 388.7 %copy-start = (bf16[1,1440,360]{2,1,0:T(8,128)(2,1)S(1)}, bf16[1,1440,360]{2,1,0:T(8,128)(2,1)}, u32[]{:S(2)}) copy-start(bf16[1,1440,360]{2,1,0:T(8,128)(2,1)} %param.16) | copy-start | bytes 3110404
  7.2 1.0 copy-start.1
  8.2 5.7 copy-start.5
  51.6 290.0 %all-to-all-start = ((bf16[64,16,2880]{2,1,0:T(8,128)(2,1)}), bf16[64,16,2880]{2,1,0:T(8,128)(2,1)}, u32[]{:S(2)}, u32[]{:S(2)}) async-start(bf16[64,16,2880]{2,1,0:T(8,128)(2,1)} %broadcast_select_fusion), calls=%async_computation | async-start | bytes 12058624 | tf_op jit(solution)/shard_map/all_to_all | solution.py:54
  76.4 315.1 %all-gather.9.cloned.1.call-start = ((), (), s32[]{:S(2)}) async-start(), calls=%async_computation.3 | async-start | bytes 3391488 | tf_op jit(solution)/shard_map/all_gather | solution.py:65
  348.5 256.9 %all-gather.11.cloned.1.call-start = ((), (), s32[]{:S(2)}) async-start(), calls=%async_computation.4 | async-start | bytes 1597440 | tf_op jit(solution)/shard_map/all_gather | solution.py:89
  349.2 334.4 %all-gather.13.cloned.1.call-start = ((), (), s32[]{:S(2)}) async-start(), calls=%async_computation.5 | async-start | bytes 1597440 | tf_op jit(solution)/shard_map/all_gather | solution.py:139
  399.1 19.8 %copy-start.12 = (f32[128,4]{0,1:T(4,128)S(1)}, f32[128,4]{0,1:T(4,128)}, u32[]{:S(2)}) copy-start(f32[128,4]{0,1:T(4,128)} %param.13) | copy-start | bytes 6148
  399.1 19.9 %copy-start.7 = (bf16[45,64]{1,0:T(8,128)(2,1)S(1)}, bf16[45,64]{1,0:T(8,128)(2,1)}, u32[]{:S(2)}) copy-start(bf16[45,64]{1,0:T(8,128)(2,1)} %param.19) | copy-start | bytes 17284
  399.1 128.5 %copy-start.8 = (bf16[45,64]{1,0:T(8,128)(2,1)S(1)}, bf16[45,64]{1,0:T(8,128)(2,1)}, u32[]{:S(2)}) copy-start(bf16[45,64]{1,0:T(8,128)(2,1)} %param.20) | copy-start | bytes 17284
  400.3 285.7 %all-to-all-start.1 = ((bf16[64,16,360]{2,1,0:T(8,128)(2,1)}), bf16[64,16,360]{2,1,0:T(8,128)(2,1)S(1)}, u32[]{:S(2)}, u32[]{:S(2)}) async-start(bf16[64,16,360]{2,1,0:T(8,128)(2,1)} %bitcast.9), calls=%async_computation.1 | async-start | bytes 1572864 | tf_op jit(solution)/shard_map/all_to_all | solution.py:68
  418.7 424.2 %reduce-scatter.5.cloned.1.call-start = ((), (), s32[]{:S(2)}) async-start(), calls=%async_computation.6 | async-start | bytes 829440
  603.4 5.4 copy-start.9
  603.4 5.3 copy-start.11
  688.6 43.4 %copy-start.10 = (f32[32]{0:T(128)S(1)}, f32[32]{0:T(128)}, u32[]{:S(2)}) copy-start(f32[32]{0:T(128)} %copy-done.9) | copy-start | bytes 388
  690.3 82.1 %copy-start.6 = (f32[128,32]{0,1:T(8,128)S(1)}, f32[128,32]{0,1:T(8,128)}, u32[]{:S(2)}) copy-start(f32[128,32]{0,1:T(8,128)} %get-tuple-element.15) | copy-start | bytes 49156
  690.5 82.0 %copy-start.4 = (pred[128,4096]{0,1:T(8,128)(4,1)S(1)}, pred[128,4096]{0,1:T(8,128)(4,1)}, u32[]{:S(2)}) copy-start(pred[128,4096]{0,1:T(8,128)(4,1)} %iota_compare_fusion) | copy-start | bytes 1572868
  705.8 66.0 %copy-start.2 = (bf16[2880,256]{1,0:T(8,128)(2,1)S(1)}, bf16[2880,256]{1,0:T(8,128)(2,1)}, u32[]{:S(2)}) copy-start(bf16[2880,256]{1,0:T(8,128)(2,1)} %reshape.319) | copy-start | bytes 4423684
  772.5 1.3 copy-start.3
Sparse Core Ops, SparseCore 0:
  348.6 42.8 all-gather.8
  394.8 148.5 all-gather.10
  546.7 136.7 all-gather.12
  808.2 34.6 reduce-scatter.4
where the time goes:
time: 854 us; the launch traced here: 849 us
  waiting for transfers between devices  413 us (48%)
  blocking collectives  313 us (37%)
  starting transfers between devices  43.4 us (5%)
  local copies, waits for them, and re-layouts  34.3 us (4%)
  matrix products  16.1 us (2%)
  other arithmetic  15.2 us (2%)
  between operations  14.2 us (2%)
    all_to_all x1, waiting for transfers between devices, on_device(): lax.all_to_all(outgoing, ('section', 'expert'), split_axis=0, concat_axis...  261 us
    all_gather x1, blocking collectives, on_device(): lax.all_gather(w_key, ('section', 'expert'), axis=0, tiled=True)  107 us
    all_gather x1, waiting for transfers between devices, on_device(): lax.all_gather(w_out, ('section', 'expert'), axis=1, tiled=True)  74.8 us
    all_gather x1, blocking collectives, on_device(): lax.all_gather(w_value, ('section', 'expert'), axis=0, tiled=True)  73.9 us
    all_gather x1, waiting for transfers between devices, on_device(): all_hidden = lax.all_gather(hidden, 'tensor', axis=1, tiled=True)  41.6 us
    all_gather x1, blocking collectives, on_device(): lax.all_gather(keys, 'expert', axis=0, tiled=True)  39 us
    unnamed x5, waiting for transfers between devices  35.5 us
    all_gather x1, blocking collectives, on_device(): lax.all_gather(values, 'expert', axis=0, tiled=True)  28.5 us
  transfers between devices with their start and end apart: 6, of which 4 were waited for; matrix products, arithmetic and copies ran while one was open for 3% of the time, Pallas kernels for 0%

commit v1 on v0

v1 whole, which is shorter than its diff:
```python
import math

import jax
import jax.numpy as jnp
from jax import lax
from jax.sharding import Mesh
from jax.sharding import PartitionSpec as P

HD = 64
EPSILON = 1e-05
GROUP = ("section", "z", "core")
TENSOR = ("xlo", "y")


def gather_rows(x, axes, count):
    copies = jnp.broadcast_to(x[None], (count,) + x.shape)
    gathered = lax.all_to_all(copies, axes, split_axis=0, concat_axis=0, tiled=True)
    return gathered.reshape((count * x.shape[0],) + x.shape[1:])


def route(expert_ids, gates, remap, groups, capacity):
    token_rows, topk = expert_ids.shape
    experts = jnp.arange(groups, dtype=jnp.int32)
    hit = expert_ids[:, :, None] == experts
    physical = jnp.sum(jnp.where(hit, remap, 0), axis=2)
    picked = physical[:, :, None] == experts
    chosen = jnp.any(picked, axis=1)
    gate = jnp.sum(jnp.where(picked, gates[:, :, None], 0.0), axis=1)
    order = jnp.arange(token_rows, dtype=jnp.int32)
    before = (order[None, :] < order[:, None]).astype(jnp.bfloat16)
    rank = jnp.dot(before, chosen.astype(jnp.bfloat16), preferred_element_type=jnp.float32)
    tag = jnp.where(chosen, rank + 1.0, 0.0).astype(jnp.bfloat16)
    slots = jnp.arange(groups * capacity, dtype=jnp.int32)
    spread = (experts[:, None] == slots[None, :] // capacity).astype(jnp.bfloat16)
    tag_at = jnp.dot(tag, spread, preferred_element_type=jnp.float32)
    here = tag_at == (slots % capacity + 1).astype(jnp.float32)[None, :]
    high = gate.astype(jnp.bfloat16)
    low = (gate - high.astype(jnp.float32)).astype(jnp.bfloat16)
    zero = jnp.zeros((), jnp.bfloat16)
    gate_terms = [
        jnp.where(
            here, jnp.dot(term, spread, preferred_element_type=jnp.float32).astype(jnp.bfloat16), zero
        )
        for term in (high, low)
    ]
    return here.astype(jnp.bfloat16), gate_terms


def rotate(x, cosine, sine):
    a, b = x[:, : HD // 2], x[:, HD // 2 :]
    return jnp.concatenate([a * cosine - b * sine, b * cosine + a * sine], axis=1)


def on_device(
    tokens, expert_ids, gates, remap, gate_up, down, norm_gain, w_query, w_key, w_value, w_out
):
    token_rows, slice_width = tokens.shape
    groups = lax.axis_size(GROUP)
    parts = lax.axis_size(TENSOR)
    width = parts * slice_width
    capacity = 2 * token_rows * expert_ids.shape[1] // groups
    local_hidden = gate_up.shape[2]
    query_width, kv_width = w_query.shape[1], w_key.shape[1]

    weights = lax.all_gather(
        jnp.concatenate([w_query, w_key, w_value, w_out.T], axis=1), GROUP, axis=0, tiled=True
    )

    here, gate_terms = route(expert_ids, gates, remap, groups, capacity)
    outgoing = lax.dot_general(
        here, tokens, (((0,), (0,)), ((), ())), preferred_element_type=jnp.float32
    ).astype(jnp.bfloat16)
    arrived = lax.all_to_all(
        outgoing.reshape(groups, capacity, slice_width), GROUP, split_axis=0, concat_axis=0, tiled=True
    )
    rows_in = gather_rows(arrived.reshape(groups * capacity, slice_width).T, TENSOR, parts)
    projected = jnp.dot(
        gate_up[0].reshape(2 * local_hidden, width), rows_in, preferred_element_type=jnp.float32
    )
    hidden = (jax.nn.silu(projected[:local_hidden]) * projected[local_hidden:]).astype(jnp.bfloat16)
    all_hidden = gather_rows(hidden, TENSOR, parts)
    result = lax.dot_general(
        all_hidden, down[0], (((0,), (0,)), ((), ())), preferred_element_type=jnp.float32
    ).astype(jnp.bfloat16)
    returned = lax.all_to_all(
        result.reshape(groups, capacity, slice_width), GROUP, split_axis=0, concat_axis=0, tiled=True
    ).reshape(groups * capacity, slice_width)
    mixture = sum(
        jnp.dot(term, returned, preferred_element_type=jnp.float32) for term in gate_terms
    )
    stream = (tokens.astype(jnp.float32) + mixture).astype(jnp.bfloat16)

    stream_wide = gather_rows(stream.T, TENSOR, parts).astype(jnp.float32)
    mean_square = jnp.sum(stream_wide * stream_wide, axis=0) / width
    normed = (
        stream_wide * lax.rsqrt(mean_square + EPSILON)[None, :] * norm_gain[:, None]
    ).astype(jnp.bfloat16)
    raw = lax.dot_general(
        weights[:, : query_width + 2 * kv_width],
        normed,
        (((0,), (0,)), ((), ())),
        preferred_element_type=jnp.float32,
    )
    block = lax.axis_index("z") * lax.axis_size("core") + lax.axis_index("core")
    positions = block * token_rows + jnp.arange(token_rows, dtype=jnp.int32)
    freq = jnp.exp(-math.log(150000.0) * jnp.arange(HD // 2, dtype=jnp.float32) * 2.0 / HD)
    angle = freq[:, None] * positions.astype(jnp.float32)[None, :]
    cosine, sine = jnp.cos(angle), jnp.sin(angle)
    heads_here, kv_here = query_width // HD, kv_width // HD
    per_kv = heads_here // kv_here
    queries = rotate(raw[:query_width].reshape(heads_here, HD, token_rows), cosine, sine).astype(
        jnp.bfloat16
    )
    keys = rotate(
        raw[query_width : query_width + kv_width].reshape(kv_here, HD, token_rows), cosine, sine
    ).astype(jnp.bfloat16)
    values = raw[query_width + kv_width :].reshape(kv_here, HD, token_rows).astype(jnp.bfloat16)
    both = jnp.concatenate([keys, values], axis=0).reshape(-1, token_rows)
    every = lax.all_gather(lax.all_gather(both, "z", axis=0), "core", axis=0)
    cores, planes = every.shape[:2]
    every = every.reshape(cores * planes, 2, kv_here, HD, token_rows)
    all_keys, all_values = every[:, 0], every[:, 1]
    grouped = queries.reshape(kv_here, per_kv, HD, token_rows)
    scores = (
        jnp.einsum("kgdt,bkdn->kgtbn", grouped, all_keys, preferred_element_type=jnp.float32)
        / math.sqrt(HD)
    ).reshape(kv_here, per_kv, token_rows, -1)
    key_block = (
        jnp.arange(planes, dtype=jnp.int32)[None, :] * cores
        + jnp.arange(cores, dtype=jnp.int32)[:, None]
    )
    key_positions = (
        key_block.reshape(-1, 1) * token_rows + jnp.arange(token_rows, dtype=jnp.int32)[None, :]
    ).reshape(-1)
    scores = jnp.where(key_positions[None, :] <= positions[:, None], scores, -1e30)
    top = jnp.max(scores, axis=-1, keepdims=True)
    probs = jnp.exp(scores - top)
    total = jnp.sum(probs, axis=-1)
    probs = probs.astype(jnp.bfloat16).reshape(kv_here, per_kv, token_rows, cores * planes, token_rows)
    mixed = jnp.einsum("bkdn,kgtbn->kgdt", all_values, probs, preferred_element_type=jnp.float32)
    heads = (mixed / total[:, :, None, :]).astype(jnp.bfloat16).reshape(query_width, token_rows)

    partial_out = jnp.dot(
        weights[:, query_width + 2 * kv_width :], heads, preferred_element_type=jnp.float32
    ).astype(jnp.bfloat16)
    shares = lax.all_to_all(
        partial_out.reshape(parts, slice_width, token_rows), TENSOR, split_axis=0, concat_axis=0, tiled=True
    )
    attended = jnp.sum(shares.astype(jnp.float32), axis=0).astype(jnp.bfloat16).T
    return (stream, attended)


def solution(mesh):
    planes = mesh.shape["expert"] // 2
    fine = Mesh(
        mesh.devices.reshape(mesh.shape["section"], planes, 2, 2, mesh.shape["tensor"] // 2),
        GROUP + TENSOR,
    )
    return jax.shard_map(
        on_device,
        mesh=fine,
        in_specs=(
            P(GROUP, TENSOR),
            P(GROUP, None),
            P(GROUP, None),
            P(),
            P(GROUP, None, TENSOR, None),
            P(GROUP, None, TENSOR),
            P(),
            P(GROUP, TENSOR),
            P(GROUP, TENSOR),
            P(GROUP, TENSOR),
            P(TENSOR, GROUP),
        ),
        out_specs=(P(GROUP, TENSOR), P(GROUP, TENSOR)),
        check_vma=False,
    )
```

time: 854 us -> 366 us (0.43)
  waiting for transfers between devices: 413 us -> 130 us
  blocking collectives: 313 us -> 155 us
  starting transfers between devices: 43.4 us -> 18.5 us
  local copies, waits for them, and re-layouts: 34.3 us -> 20 us
  other arithmetic: 15.2 us -> 6.41 us
    all_gather x6 -> x1, blocking collectives: 298 us -> 27.9 us  [on_device(): every = lax.all_gather(lax.all_gather(both, 'z', axis=0), 'core', axis=0)]
    all_to_all x2 -> x3, waiting for transfers between devices: 261 us -> 111 us  [the longest x2 68 us: gather_rows(): lax.all_to_all(copies, axes, split_axis=0, concat_axis=0, tiled=True)]
    all_to_all x0 -> x3, blocking collectives: none -> 127 us  [the longest x1 61.5 us: on_device(): lax.all_to_all(outgoing.reshape(groups, capacity, slice_width), GROUP, sp...]
    all_gather x3 -> x2, waiting for transfers between devices: 116 us -> 19.3 us  [the longest x1 19.3 us: on_device(): every = lax.all_gather(lax.all_gather(both, 'z', axis=0), 'core', axis=0)]
    unnamed x5 -> x2, waiting for transfers between devices: 35.5 us -> 0.03 us
    all_to_all x2 -> x3, starting transfers between devices: 43.2 us -> 18.2 us  [the longest x1 9.83 us: on_device(): lax.all_to_all(result.reshape(groups, capacity, slice_width), GROUP, spli...]
    psum x1 -> x0, blocking collectives: 15.1 us -> none  [on_device(): squares = lax.psum(jnp.sum(stream_wide * stream_wide, axis=1), 'tensor')]
    gather x3 -> x0, local copies, waits for them, and re-layouts: 12.5 us -> none  [the longest x1 6.57 us: on_device(): whole_tokens[slot_token]]
  transfers between devices with their start and end apart: 6 -> 5, of which waited for: 4 -> 4; matrix products, arithmetic and copies ran while one was open for 3% -> 8% of each run, Pallas kernels for 0% -> 0%
where the time goes in v1:
time: 366 us; the launch traced here: 364 us
  blocking collectives  155 us (42%)
  waiting for transfers between devices  130 us (36%)
  matrix products  20.4 us (6%)
  local copies, waits for them, and re-layouts  20 us (5%)
  starting transfers between devices  18.5 us (5%)
  between operations  14.4 us (4%)
  other arithmetic  6.41 us (2%)
    all_to_all x2, waiting for transfers between devices, gather_rows(): lax.all_to_all(copies, axes, split_axis=0, concat_axis=0, tiled=True)  68 us
    all_to_all x1, blocking collectives, on_device(): lax.all_to_all(outgoing.reshape(groups, capacity, slice_width), GROUP, sp...  61.5 us
    all_to_all x1, blocking collectives, gather_rows(): lax.all_to_all(copies, axes, split_axis=0, concat_axis=0, tiled=True)  50.2 us
    all_to_all x1, waiting for transfers between devices, on_device(): lax.all_to_all(result.reshape(groups, capacity, slice_width), GROUP, spli...  42.8 us
    all_gather x1, blocking collectives, on_device(): every = lax.all_gather(lax.all_gather(both, 'z', axis=0), 'core', axis=0)  27.9 us
    all_gather x1, waiting for transfers between devices, on_device(): every = lax.all_gather(lax.all_gather(both, 'z', axis=0), 'core', axis=0)  19.3 us
    all_to_all x1, blocking collectives, on_device(): lax.all_to_all(partial_out.reshape(parts, slice_width, token_rows), TENSO...  14.9 us
    all_to_all x1, starting transfers between devices, on_device(): lax.all_to_all(result.reshape(groups, capacity, slice_width), GROUP, spli...  9.83 us
  transfers between devices with their start and end apart: 5, of which 4 were waited for; matrix products, arithmetic and copies ran while one was open for 8% of the time, Pallas kernels for 0%

profile of v1, /device:TPU:1, one launch (start us, length us, event | category | flops | bytes accessed | tf_op | source)
XLA Modules:
  0.0 364.5 jit_solution(3609125567296631635)
XLA Ops:
  7.2 0.9 select_reduce_fusion.1
  8.1 0.4 convolution_compare_fusion
  8.5 1.2 convolution_convert_fusion.2
  9.8 0.4 copy.34
  10.1 61.5 %all_to_all.30 = bf16[64,16,360]{2,1,0:T(8,128)(2,1)S(1)} all-to-all(bf16[64,16,360]{2,1,0:T(8,128)(2,1)S(1)} %bitcast.77), channel_id=1, replica_groups=mesh['section'=2,'z'=16,'core'=2,'xlo'=2,'y'=4] {'section','z','core'}, dimensions={0} | all-to-all | bytes 1474560 | tf_op jit(solution)/shard_map/all_to_all | solution.py:73
  71.7 0.3 copy.35
  72.0 3.3 broadcast_in_dim.47
  75.3 4.9 %all-to-all-start.1 = ((bf16[8,360,1024]{2,1,0:T(8,128)(2,1)}), bf16[8,360,1024]{2,1,0:T(8,128)(2,1)}, u32[]{:S(2)}, u32[]{:S(2)}) async-start(bf16[8,360,1024]{2,1,0:T(8,128)(2,1)} %broadcast_in_dim.47), calls=%async_computation.1 | async-start | bytes 11796480 | tf_op jit(solution)/shard_map/all_to_all | solution.py:17
  80.2 0.0 all-gather.7.cloned.1.call-start
  80.3 0.7 maximum_bitcast_fusion.2
  81.0 0.0 all-gather.7.cloned.1.call-update
  81.0 1.8 copy.36
  82.8 2.2 reshape_squeeze.3
  85.0 61.8 %all-to-all-done.1 = bf16[8,360,1024]{2,1,0:T(8,128)(2,1)} async-done(((bf16[8,360,1024]{2,1,0:T(8,128)(2,1)}), bf16[8,360,1024]{2,1,0:T(8,128)(2,1)}, u32[]{:S(2)}, u32[]{:S(2)}) %all-to-all-start.1) | async-done | bytes 5898272 | tf_op jit(solution)/shard_map/all_to_all | solution.py:17
  146.8 5.8 %convolution_bitcast_fusion = f32[360,1024]{1,0:T(8,128)S(1)} fusion(bf16[2880,1024]{1,0:T(8,128)(2,1)} %bitcast.3, bf16[360,2880]{1,0:T(8,128)(2,1)} %reshape_squeeze.3), kind=kOutput, calls=%fused_computation.15 | convolution fusion | flops 2123366400 | bytes 9446400 | tf_op jit(solution)/shard_map/dot_general | solution.py:77
  152.6 0.2 fusion.30
  152.9 0.4 broadcast_in_dim.48
  153.2 50.2 %all_to_all.31 = bf16[8,180,1024]{2,1,0:T(8,128)(2,1)} all-to-all(bf16[8,180,1024]{2,1,0:T(8,128)(2,1)S(1)} %broadcast_in_dim.48), channel_id=1, replica_groups=mesh['section'=2,'z'=16,'core'=2,'xlo'=2,'y'=4] {'xlo','y'}, dimensions={0} | all-to-all | bytes 5898240 | tf_op jit(solution)/shard_map/all_to_all | solution.py:17
  203.4 4.4 %reshape.342 = bf16[1440,1024]{1,0:T(8,128)(2,1)} reshape(bf16[8,180,1024]{2,1,0:T(8,128)(2,1)} %all_to_all.31) | data formatting | bytes 5898240 | tf_op jit(solution)/shard_map/reshape | solution.py:18
  207.8 3.2 convolution_convert_fusion.1
  211.0 1.2 copy.37
  212.2 9.8 %all-to-all-start.3 = ((bf16[64,16,360]{2,1,0:T(8,128)(2,1)}), bf16[64,16,360]{2,1,0:T(8,128)(2,1)S(1)}, u32[]{:S(2)}, u32[]{:S(2)}) async-start(bf16[64,16,360]{2,1,0:T(8,128)(2,1)} %bitcast.6), calls=%async_computation.3 | async-start | bytes 1572864 | tf_op jit(solution)/shard_map/all_to_all | solution.py:85
  222.0 42.8 %all-to-all-done.3 = bf16[64,16,360]{2,1,0:T(8,128)(2,1)S(1)} async-done(((bf16[64,16,360]{2,1,0:T(8,128)(2,1)}), bf16[64,16,360]{2,1,0:T(8,128)(2,1)S(1)}, u32[]{:S(2)}, u32[]{:S(2)}) %all-to-all-start.3) | async-done | bytes 737312 | tf_op jit(solution)/shard_map/all_to_all | solution.py:85
  264.9 0.6 fusion.12
  265.5 0.6 fusion.17
  266.1 1.0 broadcast_in_dim.50
  267.0 3.5 all-to-all-start.4
  270.6 0.2 all-gather.5.cloned.1.call-start
  270.9 0.0 all-gather.7.cloned.1.call-done
  270.9 4.9 %reshape.356 = bf16[2880,640]{1,0:T(8,128)(2,1)} reshape(bf16[64,45,640]{2,1,0:T(8,128)(2,1)} %all-gather.7.cloned.1.call-done) | data formatting | bytes 7372800
  275.8 6.2 %all-to-all-done.4 = bf16[8,360,128]{2,1,0:T(8,128)(2,1)S(1)} async-done(((bf16[8,360,128]{2,1,0:T(8,128)(2,1)}), bf16[8,360,128]{2,1,0:T(8,128)(2,1)S(1)}, u32[]{:S(2)}, u32[]{:S(2)}) %all-to-all-start.4) | async-done | bytes 737312 | tf_op jit(solution)/shard_map/all_to_all | solution.py:17
  282.1 0.4 multiply_reduce_fusion
  282.5 0.4 fusion.10
  282.9 2.4 fusion.6
  285.4 0.1 fusion.47
  285.6 27.9 %all_gather.13 = bf16[16,128,128]{2,1,0:T(8,128)(2,1)} all-gather(bf16[1,128,128]{2,1,0:T(8,128)(2,1)S(1)} %bitcast.82), channel_id=1, replica_groups=mesh['section'=2,'z'=16,'core'=2,'xlo'=2,'y'=4] {'z'}, dimensions={0}, use_global_device_ids=true | all-gather | bytes 557056 | tf_op jit(solution)/shard_map/all_gather | solution.py:119
  313.5 0.0 all-gather.5.cloned.1.call-update
  313.6 0.1 mul.137
  313.6 0.1 iota_add_fusion
  313.7 0.1 multiply_cosine_fusion.1
  313.9 0.7 broadcast_compare_fusion
  314.6 19.3 %all-gather.5.cloned.1.call-done = bf16[32,128,128]{2,1,0:T(8,128)(2,1)} async-done(((bf16[16,128,128]{2,1,0:T(8,128)(2,1)}), bf16[32,128,128]{2,1,0:T(8,128)(2,1)}) %all-gather.5.cloned.1.call-update) | async-done | bytes 1048592 | tf_op jit(solution)/shard_map/all_gather | solution.py:119
  334.0 2.3 fusion
  336.3 1.8 fusion.1
  338.2 1.9 fusion.27
  340.1 1.9 convolution_convert_fusion
  342.0 14.9 %all_to_all.32 = bf16[8,360,128]{2,1,0:T(8,128)(2,1)S(1)} all-to-all(bf16[8,360,128]{2,1,0:T(8,128)(2,1)S(1)} %bitcast.79), channel_id=1, replica_groups=mesh['section'=2,'z'=16,'core'=2,'xlo'=2,'y'=4] {'xlo','y'}, dimensions={0} | all-to-all | bytes 1474560 | tf_op jit(solution)/shard_map/all_to_all | solution.py:146
  356.9 0.7 reduce_sum.52
  (34 shorter events, 0.2 us)
Async XLA Ops:
  7.2 200.6 %copy-start = (bf16[1,1440,360]{2,1,0:T(8,128)(2,1)S(1)}, bf16[1,1440,360]{2,1,0:T(8,128)(2,1)}, u32[]{:S(2)}) copy-start(bf16[1,1440,360]{2,1,0:T(8,128)(2,1)} %param.16) | copy-start | bytes 3110404
  75.3 4.9 %copy-start.3 = (bf16[256,45]{0,1:T(8,128)(2,1)S(1)}, bf16[256,45]{0,1:T(8,128)(2,1)}, u32[]{:S(2)}) copy-start(bf16[256,45]{0,1:T(8,128)(2,1)} %param.21) | copy-start | bytes 69124
  75.3 4.9 %copy-start.4 = (bf16[45,256]{1,0:T(8,128)(2,1)S(1)}, bf16[45,256]{1,0:T(8,128)(2,1)}, u32[]{:S(2)}) copy-start(bf16[45,256]{1,0:T(8,128)(2,1)} %param.18) | copy-start | bytes 69124
  75.3 4.9 %copy-start.6 = (bf16[45,64]{1,0:T(8,128)(2,1)S(1)}, bf16[45,64]{1,0:T(8,128)(2,1)}, u32[]{:S(2)}) copy-start(bf16[45,64]{1,0:T(8,128)(2,1)} %param.20) | copy-start | bytes 17284
  75.3 5.0 %copy-start.7 = (bf16[45,64]{1,0:T(8,128)(2,1)S(1)}, bf16[45,64]{1,0:T(8,128)(2,1)}, u32[]{:S(2)}) copy-start(bf16[45,64]{1,0:T(8,128)(2,1)} %param.19) | copy-start | bytes 17284
  75.3 71.5 %all-to-all-start.1 = ((bf16[8,360,1024]{2,1,0:T(8,128)(2,1)}), bf16[8,360,1024]{2,1,0:T(8,128)(2,1)}, u32[]{:S(2)}, u32[]{:S(2)}) async-start(bf16[8,360,1024]{2,1,0:T(8,128)(2,1)} %broadcast_in_dim.47), calls=%async_computation.1 | async-start | bytes 11796480 | tf_op jit(solution)/shard_map/all_to_all | solution.py:17
  80.2 190.7 %all-gather.7.cloned.1.call-start = ((), (), s32[]{:S(2)}) async-start(), calls=%async_computation.7 | async-start | bytes 3993600 | tf_op jit(solution)/shard_map/all_gather | solution.py:65
  211.0 11.0 %copy-start.8 = (f32[128,4]{0,1:T(4,128)S(1)}, f32[128,4]{0,1:T(4,128)}, u32[]{:S(2)}) copy-start(f32[128,4]{0,1:T(4,128)} %param.13) | copy-start | bytes 6148
  211.0 54.5 %copy-start.2 = (bf16[128,360]{0,1:T(8,128)(2,1)S(1)}, bf16[128,360]{0,1:T(8,128)(2,1)}, u32[]{:S(2)}) copy-start(bf16[128,360]{0,1:T(8,128)(2,1)} %param.11) | copy-start | bytes 276484
  212.2 52.7 %all-to-all-start.3 = ((bf16[64,16,360]{2,1,0:T(8,128)(2,1)}), bf16[64,16,360]{2,1,0:T(8,128)(2,1)S(1)}, u32[]{:S(2)}, u32[]{:S(2)}) async-start(bf16[64,16,360]{2,1,0:T(8,128)(2,1)} %bitcast.6), calls=%async_computation.3 | async-start | bytes 1572864 | tf_op jit(solution)/shard_map/all_to_all | solution.py:85
  266.1 9.8 %copy-start.1 = (bf16[128,360]{0,1:T(8,128)(2,1)}, bf16[128,360]{0,1:T(8,128)(2,1)S(1)}, u32[]{:S(2)}) copy-start(bf16[128,360]{0,1:T(8,128)(2,1)S(1)} %fusion.17) | copy-start | bytes 276484
  267.0 15.1 %all-to-all-start.4 = ((bf16[8,360,128]{2,1,0:T(8,128)(2,1)}), bf16[8,360,128]{2,1,0:T(8,128)(2,1)S(1)}, u32[]{:S(2)}, u32[]{:S(2)}) async-start(bf16[8,360,128]{2,1,0:T(8,128)(2,1)} %broadcast_in_dim.50), calls=%async_computation.4 | async-start | bytes 1474560 | tf_op jit(solution)/shard_map/all_to_all | solution.py:17
  270.6 63.4 %all-gather.5.cloned.1.call-start = ((), (), s32[]{:S(2)}) async-start(), calls=%async_computation.6 | async-start | bytes 1572864 | tf_op jit(solution)/shard_map/all_gather | solution.py:119
  270.9 11.6 %copy-start.5 = (f32[2880]{0:T(1024)S(1)}, f32[2880]{0:T(1024)}, u32[]{:S(2)}) copy-start(f32[2880]{0:T(1024)} %param.17) | copy-start | bytes 34564
  336.3 1.8 copy-start.9
Sparse Core Ops, SparseCore 0:
  84.8 160.6 all-gather.6
  313.7 20.2 all-gather.4

commit v2 on v1

--- a/solution.py
+++ b/solution.py
@@ -43,7 +43,9 @@
         )
         for term in (high, low)
     ]
-    return here.astype(jnp.bfloat16), gate_terms
+    count = jnp.sum(chosen.astype(jnp.float32), axis=0)
+    heavy = (count > capacity // 2).astype(jnp.bfloat16)
+    return here.astype(jnp.bfloat16), heavy, gate_terms
 
 
 def rotate(x, cosine, sine):
@@ -62,26 +64,83 @@
     local_hidden = gate_up.shape[2]
     query_width, kv_width = w_query.shape[1], w_key.shape[1]
 
+    share = w_query.shape[0]
+    fill = -share % 8
     weights = lax.all_gather(
-        jnp.concatenate([w_query, w_key, w_value, w_out.T], axis=1), GROUP, axis=0, tiled=True
-    )
-
-    here, gate_terms = route(expert_ids, gates, remap, groups, capacity)
+        jnp.pad(
+            jnp.concatenate([w_query, w_key, w_value, w_out.T], axis=1), ((0, fill), (0, 0))
+        ),
+        GROUP,
+        axis=0,
+        tiled=True,
+    )
+
+    def filled(x):
+        return jnp.pad(
+            x.reshape(-1, share, x.shape[1]), ((0, 0), (0, fill), (0, 0))
+        ).reshape(-1, x.shape[1])
+
+    here, heavy, gate_terms = route(expert_ids, gates, remap, groups, capacity)
     outgoing = lax.dot_general(
         here, tokens, (((0,), (0,)), ((), ())), preferred_element_type=jnp.float32
     ).astype(jnp.bfloat16)
-    arrived = lax.all_to_all(
-        outgoing.reshape(groups, capacity, slice_width), GROUP, split_axis=0, concat_axis=0, tiled=True
-    )
-    rows_in = gather_rows(arrived.reshape(groups * capacity, slice_width).T, TENSOR, parts)
-    projected = jnp.dot(
-        gate_up[0].reshape(2 * local_hidden, width), rows_in, preferred_element_type=jnp.float32
-    )
-    hidden = (jax.nn.silu(projected[:local_hidden]) * projected[local_hidden:]).astype(jnp.bfloat16)
-    all_hidden = gather_rows(hidden, TENSOR, parts)
-    result = lax.dot_general(
-        all_hidden, down[0], (((0,), (0,)), ((), ())), preferred_element_type=jnp.float32
-    ).astype(jnp.bfloat16)
+    per_slot = groups // capacity
+    flags = jnp.broadcast_to(heavy.reshape(1, capacity, per_slot), (groups, capacity, per_slot))
+    outgoing = jnp.concatenate([outgoing.reshape(groups, capacity, slice_width), flags], axis=2)
+    arrived = lax.all_to_all(outgoing, GROUP, split_axis=0, concat_axis=0, tiled=True)
+    flags = arrived[:, :, slice_width:].astype(jnp.float32)
+    arrived = arrived[:, :, :slice_width].reshape(groups * capacity, slice_width)
+
+    half = capacity // 2
+    spare = groups * capacity // 8
+    me = lax.axis_index(GROUP)
+    listed = (
+        jnp.arange(capacity, dtype=jnp.int32)[:, None] * per_slot
+        + jnp.arange(per_slot, dtype=jnp.int32)[None, :]
+    )
+    mine = jnp.sum(jnp.where(listed == me, flags, 0.0), axis=(1, 2)).astype(jnp.int32)
+    fits = jnp.max(jnp.sum(flags, axis=0)) * half <= spare
+    group_order = jnp.arange(groups, dtype=jnp.int32)
+    earlier = jnp.sum(jnp.where(group_order[None, :] < group_order[:, None], mine[None, :], 0), axis=1)
+
+    padding = -local_hidden % 8
+    into = jnp.pad(gate_up[0], ((0, 0), (0, padding), (0, 0))).reshape(-1, width)
+    out_of = jnp.pad(
+        down[0].reshape(parts, local_hidden, slice_width), ((0, 0), (0, padding), (0, 0))
+    ).reshape(-1, slice_width)
+
+    def expert(columns):
+        rows_in = gather_rows(columns, TENSOR, parts)
+        projected = jnp.dot(into, rows_in, preferred_element_type=jnp.float32)
+        split = local_hidden + padding
+        hidden = (jax.nn.silu(projected[:split]) * projected[split:]).astype(jnp.bfloat16)
+        return lax.dot_general(
+            gather_rows(hidden, TENSOR, parts),
+            out_of,
+            (((0,), (0,)), ((), ())),
+            preferred_element_type=jnp.float32,
+        ).astype(jnp.bfloat16)
+
+    def compact(arrived):
+        slot = jnp.arange(capacity, dtype=jnp.int32)[None, :]
+        extra = groups * half + half * earlier[:, None] + slot - half
+        place = jnp.where(
+            slot < half,
+            half * group_order[:, None] + slot,
+            jnp.where(mine[:, None] > 0, extra, -1),
+        )
+        kept = groups * half + spare
+        keep = (
+            (place[:, :, None] == jnp.arange(kept, dtype=jnp.int32))
+            .astype(jnp.bfloat16)
+            .reshape(groups * capacity, kept)
+        )
+        columns = lax.dot_general(
+            arrived, keep, (((0,), (0,)), ((), ())), preferred_element_type=jnp.float32
+        ).astype(jnp.bfloat16)
+        return jnp.dot(keep, expert(columns), preferred_element_type=jnp.float32).astype(jnp.bfloat16)
+
+    result = lax.cond(fits, compact, lambda arrived: expert(arrived.T), arrived)
     returned = lax.all_to_all(
         result.reshape(groups, capacity, slice_width), GROUP, split_axis=0, concat_axis=0, tiled=True
     ).reshape(groups * capacity, slice_width)
@@ -90,10 +149,10 @@
     )
     stream = (tokens.astype(jnp.float32) + mixture).astype(jnp.bfloat16)
 
-    stream_wide = gather_rows(stream.T, TENSOR, parts).astype(jnp.float32)
+    stream_wide = gather_rows(filled(stream.T), TENSOR, parts).astype(jnp.float32)
     mean_square = jnp.sum(stream_wide * stream_wide, axis=0) / width
     normed = (
-        stream_wide * lax.rsqrt(mean_square + EPSILON)[None, :] * norm_gain[:, None]
+        stream_wide * lax.rsqrt(mean_square + EPSILON)[None, :] * filled(norm_gain[:, None])
     ).astype(jnp.bfloat16)
     raw = lax.dot_general(
         weights[:, : query_width + 2 * kv_width],
@@ -116,9 +175,10 @@
     ).astype(jnp.bfloat16)
     values = raw[query_width + kv_width :].reshape(kv_here, HD, token_rows).astype(jnp.bfloat16)
     both = jnp.concatenate([keys, values], axis=0).reshape(-1, token_rows)
-    every = lax.all_gather(lax.all_gather(both, "z", axis=0), "core", axis=0)
-    cores, planes = every.shape[:2]
-    every = every.reshape(cores * planes, 2, kv_here, HD, token_rows)
+    own = lax.all_gather(both, "z", axis=0)
+    cores, planes = lax.axis_size("core"), own.shape[0]
+    other = lax.ppermute(own, "core", [(i, (i + 1) % cores) for i in range(cores)])
+    every = jnp.concatenate([own, other], axis=0).reshape(cores * planes, 2, kv_here, HD, token_rows)
     all_keys, all_values = every[:, 0], every[:, 1]
     grouped = queries.reshape(kv_here, per_kv, HD, token_rows)
     scores = (
@@ -127,7 +187,7 @@
     ).reshape(kv_here, per_kv, token_rows, -1)
     key_block = (
         jnp.arange(planes, dtype=jnp.int32)[None, :] * cores
-        + jnp.arange(cores, dtype=jnp.int32)[:, None]
+        + (jnp.arange(cores, dtype=jnp.int32)[:, None] + lax.axis_index("core")) % cores
     )
     key_positions = (
         key_block.reshape(-1, 1) * token_rows + jnp.arange(token_rows, dtype=jnp.int32)[None, :]
@@ -144,9 +204,11 @@
         weights[:, query_width + 2 * kv_width :], heads, preferred_element_type=jnp.float32
     ).astype(jnp.bfloat16)
     shares = lax.all_to_all(
-        partial_out.reshape(parts, slice_width, token_rows), TENSOR, split_axis=0, concat_axis=0, tiled=True
-    )
-    attended = jnp.sum(shares.astype(jnp.float32), axis=0).astype(jnp.bfloat16).T
+        partial_out.reshape(parts, -1, token_rows), TENSOR, split_axis=0, concat_axis=0, tiled=True
+    )
+    attended = jnp.sum(shares.astype(jnp.float32), axis=0).astype(jnp.bfloat16)
+    attended = attended.reshape(-1, share + fill, token_rows)[:, :share]
+    attended = attended.reshape(slice_width, token_rows).T
     return (stream, attended)
 
 

time: 366 us -> 311 us (0.85)
  blocking collectives: 155 us -> 117 us
  waiting for transfers between devices: 130 us -> 92.4 us
  starting transfers between devices: 18.5 us -> 47.9 us
  local copies, waits for them, and re-layouts: 20 us -> 10.4 us
    all_to_all x2 -> x1, blocking collectives: 76.4 us -> 15 us  [on_device(): lax.all_to_all(partial_out.reshape(parts, -1, token_rows), TENSOR, split_...]
    all_to_all x2 -> x1, waiting for transfers between devices: 68 us -> 11.8 us  [gather_rows(): lax.all_to_all(copies, axes, split_axis=0, concat_axis=0, tiled=True)]
    all_to_all x0 -> x1, waiting for transfers between devices: none -> 37.9 us  [on_device(): lax.all_to_all(outgoing, GROUP, split_axis=0, concat_axis=0, tiled=True)]
    all_to_all x1 -> x2, blocking collectives: 50.2 us -> 76.2 us  [gather_rows(): lax.all_to_all(copies, axes, split_axis=0, concat_axis=0, tiled=True)]
    all_to_all x0 -> x1, starting transfers between devices: none -> 19.8 us  [on_device(): lax.all_to_all(outgoing, GROUP, split_axis=0, concat_axis=0, tiled=True)]
    all_gather x2 -> x1, waiting for transfers between devices: 19.3 us -> 0.02 us  [on_device(): lax.all_gather(jnp.pad(jnp.concatenate([w_query, w_key, w_value, w_out.T]...]
    ppermute x0 -> x1, starting transfers between devices: none -> 9.47 us  [on_device(): lax.ppermute(own, 'core', [(i, (i + 1) % cores) for i in range(cores)])]
    all_to_all x1, starting transfers between devices: 9.83 us -> 15.1 us  [on_device(): lax.all_to_all(result.reshape(groups, capacity, slice_width), GROUP, spli...]
  transfers between devices with their start and end apart: 5 -> 5, of which waited for: 4 -> 4; matrix products, arithmetic and copies ran while one was open for 8% -> 7% of each run, Pallas kernels for 0% -> 0%
where the time goes in v2:
time: 311 us; the launch traced here: 310 us
  blocking collectives  117 us (38%)
  waiting for transfers between devices  92.4 us (30%)
  starting transfers between devices  47.9 us (15%)
  matrix products  17.6 us (6%)
  between operations  15.1 us (5%)
  local copies, waits for them, and re-layouts  10.4 us (3%)
  other arithmetic  9.96 us (3%)
    all_to_all x2, blocking collectives, gather_rows(): lax.all_to_all(copies, axes, split_axis=0, concat_axis=0, tiled=True)  76.2 us
    all_to_all x1, waiting for transfers between devices, on_device(): lax.all_to_all(result.reshape(groups, capacity, slice_width), GROUP, spli...  42 us
    all_to_all x1, waiting for transfers between devices, on_device(): lax.all_to_all(outgoing, GROUP, split_axis=0, concat_axis=0, tiled=True)  37.9 us
    all_gather x1, blocking collectives, on_device(): own = lax.all_gather(both, 'z', axis=0)  25.4 us
    all_to_all x1, starting transfers between devices, on_device(): lax.all_to_all(outgoing, GROUP, split_axis=0, concat_axis=0, tiled=True)  19.8 us
    all_to_all x1, starting transfers between devices, on_device(): lax.all_to_all(result.reshape(groups, capacity, slice_width), GROUP, spli...  15.1 us
    all_to_all x1, blocking collectives, on_device(): lax.all_to_all(partial_out.reshape(parts, -1, token_rows), TENSOR, split_...  15 us
    all_to_all x1, waiting for transfers between devices, gather_rows(): lax.all_to_all(copies, axes, split_axis=0, concat_axis=0, tiled=True)  11.8 us
  transfers between devices with their start and end apart: 5, of which 4 were waited for; matrix products, arithmetic and copies ran while one was open for 7% of the time, Pallas kernels for 0%

profile of v2, /device:TPU:1, one launch (start us, length us, event | category | flops | bytes accessed | tf_op | source)
XLA Modules:
  0.0 310.2 jit_solution(3080611906285902582)
XLA Ops:
  7.2 0.8 select_reduce_fusion.2
  8.1 0.4 convolution_compare_fusion
  8.5 1.2 convolution_convert_fusion.2
  9.8 0.4 copy.46
  10.4 1.1 pad_maximum_fusion.1
  11.4 19.8 %all-to-all-start.4 = ((bf16[64,16,364]{2,1,0:T(8,128)(2,1)}), bf16[64,16,364]{2,1,0:T(8,128)(2,1)}, u32[]{:S(2)}, u32[]{:S(2)}) async-start(bf16[64,16,364]{2,1,0:T(8,128)(2,1)} %pad_maximum_fusion.1), calls=%async_computation.4 | async-start | bytes 1572864 | tf_op jit(solution)/shard_map/all_to_all | solution.py:90
  31.3 0.7 fusion.55
  32.0 1.8 copy.59
  33.9 1.4 reshape_squeeze.3
  35.2 1.5 pad.20.clone
  36.8 0.1 pad.21
  37.0 37.9 %all-to-all-done.4 = bf16[64,16,364]{2,1,0:T(8,128)(2,1)} async-done(((bf16[64,16,364]{2,1,0:T(8,128)(2,1)}), bf16[64,16,364]{2,1,0:T(8,128)(2,1)}, u32[]{:S(2)}, u32[]{:S(2)}) %all-to-all-start.4) | async-done | bytes 745504 | tf_op jit(solution)/shard_map/all_to_all | solution.py:90
  74.9 1.9 fusion.37
  76.8 0.6 reduce_max.18
  78.1 84.6 %conditional.2 = (bf16[1024,360]{0,1:T(8,128)(2,1)}) conditional(s32[]{:T(128)} %convert_element_type.159, (bf16[1024,360]{1,0:T(8,128)(2,1)}, bf16[368,2880]{1,0:T(8,128)(2,1)}, bf16[1472,360]{1,0:T(8,128)(2,1)S(1)}) %tuple.32, (s32[64]{0:T(128)S(1)}, s32[64]{0:T(128)S(1)}, s32[64,64]{1,0:T(8,128)S(1)}, s32[64,64]{1,0:T(8,128)S(1)}, ...), branch_computations={%region_7.8_spmd, %region_8.10_spmd} | conditional | flops 3256958976 | bytes 54027300
  78.8 2.1 fusion.6
  80.8 0.3 broadcast_in_dim.87
  81.2 48.7 %all_to_all.38 = bf16[8,360,640]{2,1,0:T(8,128)(2,1)S(1)} all-to-all(bf16[8,360,640]{2,1,0:T(8,128)(2,1)S(1)} %broadcast_in_dim.87), channel_id=1, replica_groups=mesh['section'=2,'z'=16,'core'=2,'xlo'=2,'y'=4] {'xlo','y'}, dimensions={0} | all-to-all | bytes 7372800 | tf_op jit(solution)/shard_map/cond/branch_1_fun/all_to_all | solution.py:17
  129.8 1.9 convolution_bitcast_fusion
  131.8 0.1 fusion.7
  131.9 0.1 broadcast_in_dim.88
  132.1 27.5 %all_to_all.39 = bf16[8,184,640]{2,1,0:T(8,128)(2,1)S(1)} all-to-all(bf16[8,184,640]{2,1,0:T(8,128)(2,1)S(1)} %broadcast_in_dim.88), channel_id=1, replica_groups=mesh['section'=2,'z'=16,'core'=2,'xlo'=2,'y'=4] {'xlo','y'}, dimensions={0} | all-to-all | bytes 3768320 | tf_op jit(solution)/shard_map/cond/branch_1_fun/all_to_all | solution.py:17
  159.6 3.1 fusion.1
  162.7 2.3 copy.49
  165.0 15.1 %all-to-all-start.5 = ((bf16[64,16,360]{2,1,0:T(8,128)(2,1)}), bf16[64,16,360]{2,1,0:T(8,128)(2,1)S(1)}, u32[]{:S(2)}, u32[]{:S(2)}) async-start(bf16[64,16,360]{2,1,0:T(8,128)(2,1)} %bitcast.12), calls=%async_computation.5 | async-start | bytes 1572864 | tf_op jit(solution)/shard_map/all_to_all | solution.py:144
  180.2 42.0 %all-to-all-done.5 = bf16[64,16,360]{2,1,0:T(8,128)(2,1)S(1)} async-done(((bf16[64,16,360]{2,1,0:T(8,128)(2,1)}), bf16[64,16,360]{2,1,0:T(8,128)(2,1)S(1)}, u32[]{:S(2)}, u32[]{:S(2)}) %all-to-all-start.5) | async-done | bytes 737312 | tf_op jit(solution)/shard_map/all_to_all | solution.py:144
  222.2 0.6 fusion.20
  222.8 0.6 fusion.25
  223.4 1.0 broadcast_in_dim.167
  224.4 3.5 %all-to-all-start.6 = ((bf16[8,384,128]{2,1,0:T(8,128)(2,1)}), bf16[8,384,128]{2,1,0:T(8,128)(2,1)S(1)}, u32[]{:S(2)}, u32[]{:S(2)}) async-start(bf16[8,384,128]{2,1,0:T(8,128)(2,1)} %broadcast_in_dim.167), calls=%async_computation.6 | async-start | bytes 1572864 | tf_op jit(solution)/shard_map/all_to_all | solution.py:17
  228.1 0.1 reshape_broadcast_in_dim.3
  228.4 0.1 multiply_cosine_fusion.1
  228.6 11.8 %all-to-all-done.6 = bf16[8,384,128]{2,1,0:T(8,128)(2,1)S(1)} async-done(((bf16[8,384,128]{2,1,0:T(8,128)(2,1)}), bf16[8,384,128]{2,1,0:T(8,128)(2,1)S(1)}, u32[]{:S(2)}, u32[]{:S(2)}) %all-to-all-start.6) | async-done | bytes 786464 | tf_op jit(solution)/shard_map/all_to_all | solution.py:17
  240.4 0.4 multiply_reduce_fusion
  240.8 0.5 fusion.18
  241.3 2.5 fusion.14
  243.9 0.1 fusion.61
  244.0 25.4 %all_gather.7 = bf16[16,128,128]{2,1,0:T(8,128)(2,1)S(1)} all-gather(bf16[1,128,128]{2,1,0:T(8,128)(2,1)S(1)} %bitcast.110), channel_id=1, replica_groups=mesh['section'=2,'z'=16,'core'=2,'xlo'=2,'y'=4] {'z'}, dimensions={0}, use_global_device_ids=true | all-gather | bytes 557056 | tf_op jit(solution)/shard_map/all_gather | solution.py:178
  269.5 9.5 %collective-permute-start = (bf16[16,128,128]{2,1,0:T(8,128)(2,1)S(1)}, bf16[16,128,128]{2,1,0:T(8,128)(2,1)S(1)}, u32[]{:S(2)}, u32[]{:S(2)}) collective-permute-start(bf16[16,128,128]{2,1,0:T(8,128)(2,1)S(1)} %all_gather.7), channel_id=1, source_target_pairs={{0,8},{8,0},{1,9},{9,1},{2,10},{10,2},{3,11},{11,3},{4,12},{12,4},... | collective-permute-start | bytes 1572872 | tf_op jit(solution)/shard_map/ppermute | solution.py:180
  278.9 0.7 broadcast_compare_fusion.1
  279.7 0.7 collective-permute-done
  280.5 1.3 fusion.8
  281.9 1.8 fusion.9
  283.7 2.0 fusion.34
  285.6 2.0 convolution_convert_fusion.1
  287.6 15.0 %all_to_all.40 = bf16[8,384,128]{2,1,0:T(8,128)(2,1)S(1)} all-to-all(bf16[8,384,128]{2,1,0:T(8,128)(2,1)S(1)} %bitcast.105), channel_id=1, replica_groups=mesh['section'=2,'z'=16,'core'=2,'xlo'=2,'y'=4] {'xlo','y'}, dimensions={0} | all-to-all | bytes 1572864 | tf_op jit(solution)/shard_map/all_to_all | solution.py:206
  302.6 0.1 reduce_sum.92
  302.7 0.7 reshape.500
  (70 shorter events, 1.6 us)
Async XLA Ops:
  9.8 21.5 %copy-start.6 = (bf16[256,45]{0,1:T(8,128)(2,1)S(1)}, bf16[256,45]{0,1:T(8,128)(2,1)}, u32[]{:S(2)}) copy-start(bf16[256,45]{0,1:T(8,128)(2,1)} %param.23) | copy-start | bytes 69124
  9.8 21.5 %copy-start.7 = (bf16[45,256]{1,0:T(8,128)(2,1)S(1)}, bf16[45,256]{1,0:T(8,128)(2,1)}, u32[]{:S(2)}) copy-start(bf16[45,256]{1,0:T(8,128)(2,1)} %param.20) | copy-start | bytes 69124
  9.8 21.5 %copy-start.8 = (bf16[45,64]{1,0:T(8,128)(2,1)S(1)}, bf16[45,64]{1,0:T(8,128)(2,1)}, u32[]{:S(2)}) copy-start(bf16[45,64]{1,0:T(8,128)(2,1)} %param.22) | copy-start | bytes 17284
  9.8 21.5 %copy-start.9 = (bf16[45,64]{1,0:T(8,128)(2,1)S(1)}, bf16[45,64]{1,0:T(8,128)(2,1)}, u32[]{:S(2)}) copy-start(bf16[45,64]{1,0:T(8,128)(2,1)} %param.21) | copy-start | bytes 17284
  11.4 63.4 %all-to-all-start.4 = ((bf16[64,16,364]{2,1,0:T(8,128)(2,1)}), bf16[64,16,364]{2,1,0:T(8,128)(2,1)}, u32[]{:S(2)}, u32[]{:S(2)}) async-start(bf16[64,16,364]{2,1,0:T(8,128)(2,1)} %pad_maximum_fusion.1), calls=%async_computation.4 | async-start | bytes 1572864 | tf_op jit(solution)/shard_map/all_to_all | solution.py:90
  31.2 210.1 %all-gather.2.cloned.1.call-start = ((), (), s32[]{:S(2)}) async-start(), calls=%async_computation.8 | async-start | bytes 3993600 | tf_op jit(solution)/shard_map/all_gather | solution.py:69
  78.1 3.0 copy-start.2
  81.2 48.7 %copy-start.1 = (bf16[368,2880]{1,0:T(8,128)(2,1)S(1)}, bf16[368,2880]{1,0:T(8,128)(2,1)}, u32[]{:S(2)}) copy-start(bf16[368,2880]{1,0:T(8,128)(2,1)} %get-tuple-element.46) | copy-start | bytes 6359044 | tf_op jit(solution)/shard_map/conditional
  131.9 27.7 %copy-start.3 = (bf16[1472,360]{1,0:T(8,128)(2,1)S(1)}, bf16[1472,360]{1,0:T(8,128)(2,1)}, u32[]{:S(2)}) copy-start(bf16[1472,360]{1,0:T(8,128)(2,1)} %copy-done.2) | copy-start | bytes 3179524 | tf_op jit(solution)/shard_map/conditional
  162.7 17.5 %copy-start.11 = (f32[128,4]{0,1:T(4,128)S(1)}, f32[128,4]{0,1:T(4,128)}, u32[]{:S(2)}) copy-start(f32[128,4]{0,1:T(4,128)} %param.15) | copy-start | bytes 6148
  162.7 60.1 %copy-start.4 = (bf16[128,360]{0,1:T(8,128)(2,1)S(1)}, bf16[128,360]{0,1:T(8,128)(2,1)}, u32[]{:S(2)}) copy-start(bf16[128,360]{0,1:T(8,128)(2,1)} %param.13) | copy-start | bytes 276484
  165.0 57.2 %all-to-all-start.5 = ((bf16[64,16,360]{2,1,0:T(8,128)(2,1)}), bf16[64,16,360]{2,1,0:T(8,128)(2,1)S(1)}, u32[]{:S(2)}, u32[]{:S(2)}) async-start(bf16[64,16,360]{2,1,0:T(8,128)(2,1)} %bitcast.12), calls=%async_computation.5 | async-start | bytes 1572864 | tf_op jit(solution)/shard_map/all_to_all | solution.py:144
  222.2 5.9 %copy-start.10 = (f32[2880]{0:T(1024)S(1)}, f32[2880]{0:T(1024)}, u32[]{:S(2)}) copy-start(f32[2880]{0:T(1024)} %param.19) | copy-start | bytes 34564
  223.4 17.9 %copy-start.5 = (bf16[128,360]{0,1:T(8,128)(2,1)}, bf16[128,360]{0,1:T(8,128)(2,1)S(1)}, u32[]{:S(2)}) copy-start(bf16[128,360]{0,1:T(8,128)(2,1)S(1)} %fusion.25) | copy-start | bytes 276484
  224.4 16.0 %all-to-all-start.6 = ((bf16[8,384,128]{2,1,0:T(8,128)(2,1)}), bf16[8,384,128]{2,1,0:T(8,128)(2,1)S(1)}, u32[]{:S(2)}, u32[]{:S(2)}) async-start(bf16[8,384,128]{2,1,0:T(8,128)(2,1)} %broadcast_in_dim.167), calls=%async_computation.6 | async-start | bytes 1572864 | tf_op jit(solution)/shard_map/all_to_all | solution.py:17
  269.5 11.0 %collective-permute-start = (bf16[16,128,128]{2,1,0:T(8,128)(2,1)S(1)}, bf16[16,128,128]{2,1,0:T(8,128)(2,1)S(1)}, u32[]{:S(2)}, u32[]{:S(2)}) collective-permute-start(bf16[16,128,128]{2,1,0:T(8,128)(2,1)S(1)} %all_gather.7), channel_id=1, source_target_pairs={{0,8},{8,0},{1,9},{9,1},{2,10},{10,2},{3,11},{11,3},{4,12},{12,4},... | collective-permute-start | bytes 1572872 | tf_op jit(solution)/shard_map/ppermute | solution.py:180
Sparse Core Ops, SparseCore 0:
  35.8 166.9 all-gather.1

commit v3 on v2

--- a/solution.py
+++ b/solution.py
@@ -10,6 +10,7 @@
 EPSILON = 1e-05
 GROUP = ("section", "z", "core")
 TENSOR = ("xlo", "y")
+SWAP = ((0, 1), (1, 0))
 
 
 def gather_rows(x, axes, count):
@@ -66,19 +67,27 @@
 
     share = w_query.shape[0]
     fill = -share % 8
-    weights = lax.all_gather(
-        jnp.pad(
-            jnp.concatenate([w_query, w_key, w_value, w_out.T], axis=1), ((0, fill), (0, 0))
-        ),
-        GROUP,
-        axis=0,
-        tiled=True,
-    )
+    cores, planes, sections = lax.axis_size("core"), lax.axis_size("z"), lax.axis_size("section")
+    stretch = groups // parts // cores
+    second_core = lax.axis_index("core") == 1
+    partner_up = lax.ppermute(gate_up, "xlo", SWAP)
+    shard = jnp.pad(
+        jnp.concatenate([w_query, w_key, w_value, w_out.T], axis=1), ((0, fill), (0, 0))
+    )
+    across = lax.ppermute(shard, "section", SWAP)
+    pair = jnp.where(
+        lax.axis_index("section") == 0,
+        jnp.concatenate([shard, across], axis=0),
+        jnp.concatenate([across, shard], axis=0),
+    )
+
+    def own_core_first(x, axis):
+        return jnp.where(second_core, jnp.flip(x, axis), x)
 
     def filled(x):
-        return jnp.pad(
-            x.reshape(-1, share, x.shape[1]), ((0, 0), (0, fill), (0, 0))
-        ).reshape(-1, x.shape[1])
+        x = x.reshape(-1, stretch, cores, share, x.shape[1])
+        x = jnp.pad(x, ((0, 0), (0, 0), (0, 0), (0, fill), (0, 0)))
+        return own_core_first(x, 2).transpose(0, 2, 1, 3, 4).reshape(-1, x.shape[4])
 
     here, heavy, gate_terms = route(expert_ids, gates, remap, groups, capacity)
     outgoing = lax.dot_general(
@@ -88,59 +97,94 @@
     flags = jnp.broadcast_to(heavy.reshape(1, capacity, per_slot), (groups, capacity, per_slot))
     outgoing = jnp.concatenate([outgoing.reshape(groups, capacity, slice_width), flags], axis=2)
     arrived = lax.all_to_all(outgoing, GROUP, split_axis=0, concat_axis=0, tiled=True)
+    arrived, pair = lax.optimization_barrier((arrived, pair))
+    own_weights = lax.all_gather(pair, "z", axis=0, tiled=True)
     flags = arrived[:, :, slice_width:].astype(jnp.float32)
     arrived = arrived[:, :, :slice_width].reshape(groups * capacity, slice_width)
 
-    half = capacity // 2
+    halves = lax.axis_size("xlo")
+    quarter = capacity // 4
     spare = groups * capacity // 8
+    room = groups * quarter + spare
     me = lax.axis_index(GROUP)
     listed = (
         jnp.arange(capacity, dtype=jnp.int32)[:, None] * per_slot
         + jnp.arange(per_slot, dtype=jnp.int32)[None, :]
     )
     mine = jnp.sum(jnp.where(listed == me, flags, 0.0), axis=(1, 2)).astype(jnp.int32)
-    fits = jnp.max(jnp.sum(flags, axis=0)) * half <= spare
+    fits = jnp.max(jnp.sum(flags, axis=0)) * quarter <= spare
     group_order = jnp.arange(groups, dtype=jnp.int32)
     earlier = jnp.sum(jnp.where(group_order[None, :] < group_order[:, None], mine[None, :], 0), axis=1)
 
     padding = -local_hidden % 8
-    into = jnp.pad(gate_up[0], ((0, 0), (0, padding), (0, 0))).reshape(-1, width)
+    def tiled_units(weight):
+        return jnp.pad(weight[0], ((0, 0), (0, padding), (0, 0))).reshape(-1, width)
+
+    into, into_partner = tiled_units(gate_up), tiled_units(partner_up)
     out_of = jnp.pad(
         down[0].reshape(parts, local_hidden, slice_width), ((0, 0), (0, padding), (0, 0))
-    ).reshape(-1, slice_width)
-
-    def expert(columns):
-        rows_in = gather_rows(columns, TENSOR, parts)
-        projected = jnp.dot(into, rows_in, preferred_element_type=jnp.float32)
+    )
+    crossed = out_of.reshape((halves, parts // halves) + out_of.shape[1:]).transpose(1, 0, 2, 3)
+    out_of_half = [
+        turned.reshape(-1, slice_width) for turned in (crossed, jnp.flip(crossed, 1))
+    ]
+    out_of = out_of.reshape(-1, slice_width)
+
+    def hidden_units(weight, rows_in):
+        projected = jnp.dot(weight, rows_in, preferred_element_type=jnp.float32)
         split = local_hidden + padding
-        hidden = (jax.nn.silu(projected[:split]) * projected[split:]).astype(jnp.bfloat16)
+        return (jax.nn.silu(projected[:split]) * projected[split:]).astype(jnp.bfloat16)
+
+    def put_out(hidden, weight):
         return lax.dot_general(
-            gather_rows(hidden, TENSOR, parts),
-            out_of,
-            (((0,), (0,)), ((), ())),
-            preferred_element_type=jnp.float32,
+            hidden, weight, (((0,), (0,)), ((), ())), preferred_element_type=jnp.float32
         ).astype(jnp.bfloat16)
+
+    def whole(arrived):
+        rows_in = gather_rows(arrived.T, TENSOR, parts)
+        return put_out(gather_rows(hidden_units(into, rows_in), TENSOR, parts), out_of)
 
     def compact(arrived):
         slot = jnp.arange(capacity, dtype=jnp.int32)[None, :]
-        extra = groups * half + half * earlier[:, None] + slot - half
+        past = slot >= 2 * quarter
+        side = slot // quarter % 2
+        base = jnp.where(
+            past, groups * quarter + quarter * earlier[:, None], quarter * group_order[:, None]
+        )
         place = jnp.where(
-            slot < half,
-            half * group_order[:, None] + slot,
-            jnp.where(mine[:, None] > 0, extra, -1),
-        )
-        kept = groups * half + spare
+            jnp.logical_and(past, mine[:, None] == 0), -1, room * side + base + slot % quarter
+        )
         keep = (
-            (place[:, :, None] == jnp.arange(kept, dtype=jnp.int32))
+            (place[:, :, None] == jnp.arange(halves * room, dtype=jnp.int32))
             .astype(jnp.bfloat16)
-            .reshape(groups * capacity, kept)
-        )
-        columns = lax.dot_general(
-            arrived, keep, (((0,), (0,)), ((), ())), preferred_element_type=jnp.float32
-        ).astype(jnp.bfloat16)
-        return jnp.dot(keep, expert(columns), preferred_element_type=jnp.float32).astype(jnp.bfloat16)
-
-    result = lax.cond(fits, compact, lambda arrived: expert(arrived.T), arrived)
+            .reshape(groups * capacity, halves * room)
+        )
+        columns = [
+            lax.dot_general(
+                arrived,
+                keep[:, half * room : (half + 1) * room],
+                (((0,), (0,)), ((), ())),
+                preferred_element_type=jnp.float32,
+            ).astype(jnp.bfloat16)
+            for half in range(halves)
+        ]
+        copies = jnp.broadcast_to(
+            jnp.stack(columns)[:, None], (halves, parts // halves, slice_width, room)
+        )
+        rows_in = lax.all_to_all(
+            copies.reshape(parts, slice_width, room), TENSOR, split_axis=0, concat_axis=0, tiled=True
+        ).reshape(width, room)
+        hidden = jnp.concatenate(
+            [hidden_units(into, rows_in), hidden_units(into_partner, rows_in)], axis=0
+        )
+        all_hidden = gather_rows(hidden, TENSOR, parts).reshape(halves, -1, room)
+        result = jnp.concatenate(
+            [put_out(all_hidden[half], out_of_half[half]) for half in range(halves)], axis=0
+        )
+        return jnp.dot(keep, result, preferred_element_type=jnp.float32).astype(jnp.bfloat16)
+
+    result = lax.cond(fits, compact, whole, arrived)
+    other_weights = lax.ppermute(own_weights, "core", SWAP)
     returned = lax.all_to_all(
         result.reshape(groups, capacity, slice_width), GROUP, split_axis=0, concat_axis=0, tiled=True
     ).reshape(groups * capacity, slice_width)
@@ -154,11 +198,16 @@
     normed = (
         stream_wide * lax.rsqrt(mean_square + EPSILON)[None, :] * filled(norm_gain[:, None])
     ).astype(jnp.bfloat16)
-    raw = lax.dot_general(
-        weights[:, : query_width + 2 * kv_width],
-        normed,
-        (((0,), (0,)), ((), ())),
-        preferred_element_type=jnp.float32,
+    normed = normed.reshape(sections, -1, cores, stretch, share + fill, token_rows)
+    normed = normed.transpose(2, 1, 3, 0, 4, 5).reshape(cores, -1, token_rows)
+    raw = sum(
+        lax.dot_general(
+            held[:, : query_width + 2 * kv_width],
+            normed[which],
+            (((0,), (0,)), ((), ())),
+            preferred_element_type=jnp.float32,
+        )
+        for which, held in enumerate((own_weights, other_weights))
     )
     block = lax.axis_index("z") * lax.axis_size("core") + lax.axis_index("core")
     positions = block * token_rows + jnp.arange(token_rows, dtype=jnp.int32)
@@ -176,8 +225,7 @@
     values = raw[query_width + kv_width :].reshape(kv_here, HD, token_rows).astype(jnp.bfloat16)
     both = jnp.concatenate([keys, values], axis=0).reshape(-1, token_rows)
     own = lax.all_gather(both, "z", axis=0)
-    cores, planes = lax.axis_size("core"), own.shape[0]
-    other = lax.ppermute(own, "core", [(i, (i + 1) % cores) for i in range(cores)])
+    other = lax.ppermute(own, "core", SWAP)
     every = jnp.concatenate([own, other], axis=0).reshape(cores * planes, 2, kv_here, HD, token_rows)
     all_keys, all_values = every[:, 0], every[:, 1]
     grouped = queries.reshape(kv_here, per_kv, HD, token_rows)
@@ -200,15 +248,24 @@
     mixed = jnp.einsum("bkdn,kgtbn->kgdt", all_values, probs, preferred_element_type=jnp.float32)
     heads = (mixed / total[:, :, None, :]).astype(jnp.bfloat16).reshape(query_width, token_rows)
 
-    partial_out = jnp.dot(
-        weights[:, query_width + 2 * kv_width :], heads, preferred_element_type=jnp.float32
-    ).astype(jnp.bfloat16)
+    partial_out = jnp.stack(
+        [
+            jnp.dot(
+                held[:, query_width + 2 * kv_width :], heads, preferred_element_type=jnp.float32
+            ).astype(jnp.bfloat16)
+            for held in (own_weights, other_weights)
+        ]
+    ).reshape(cores, -1, stretch, sections, share + fill, token_rows)
     shares = lax.all_to_all(
-        partial_out.reshape(parts, -1, token_rows), TENSOR, split_axis=0, concat_axis=0, tiled=True
+        partial_out.transpose(3, 1, 0, 2, 4, 5).reshape(parts, -1, token_rows),
+        TENSOR,
+        split_axis=0,
+        concat_axis=0,
+        tiled=True,
     )
     attended = jnp.sum(shares.astype(jnp.float32), axis=0).astype(jnp.bfloat16)
-    attended = attended.reshape(-1, share + fill, token_rows)[:, :share]
-    attended = attended.reshape(slice_width, token_rows).T
+    attended = attended.reshape(cores, stretch, share + fill, token_rows)[:, :, :share]
+    attended = own_core_first(attended, 0).transpose(1, 0, 2, 3).reshape(slice_width, token_rows).T
     return (stream, attended)
 
 

time: 311 us -> 315 us (1.013)
  blocking collectives: 117 us -> 39.8 us
  waiting for transfers between devices: 92.4 us -> 147 us
  starting transfers between devices: 47.9 us -> 62.5 us
  local copies, waits for them, and re-layouts: 10.4 us -> 22.8 us
    all_to_all x3 -> x1, blocking collectives: 91.2 us -> 14.7 us  [on_device(): lax.all_to_all(partial_out.transpose(3, 1, 0, 2, 4, 5).reshape(parts, -1,...]
    ppermute x1 -> x4, waiting for transfers between devices: 0.73 us -> 47.6 us  [the longest x1 46.9 us: on_device(): across = lax.ppermute(shard, 'section', SWAP)]
    all_to_all x1, waiting for transfers between devices: 37.9 us -> 0.01 us  [on_device(): lax.all_to_all(outgoing, GROUP, split_axis=0, concat_axis=0, tiled=True)]
    all_to_all x0 -> x1, waiting for transfers between devices: none -> 24.2 us  [compact(): lax.all_to_all(copies.reshape(parts, slice_width, room), TENSOR, split_ax...]
    all_to_all x1 -> x2, waiting for transfers between devices: 11.8 us -> 33.8 us  [gather_rows(): lax.all_to_all(copies, axes, split_axis=0, concat_axis=0, tiled=True)]
    ppermute x1 -> x4, starting transfers between devices: 9.47 us -> 18.9 us  [the longest x1 9.31 us: on_device(): other = lax.ppermute(own, 'core', SWAP)]
    another operation x8 -> x12, local copies, waits for them, and re-layouts: 2.45 us -> 7.14 us
    all_to_all x0 -> x1, starting transfers between devices: none -> 4.18 us  [compact(): lax.all_to_all(copies.reshape(parts, slice_width, room), TENSOR, split_ax...]
  transfers between devices with their start and end apart: 5 -> 10, of which waited for: 4 -> 6; matrix products, arithmetic and copies ran while one was open for 7% -> 11% of each run, Pallas kernels for 0% -> 0%
where the time goes in v3:
time: 315 us; the launch traced here: 314 us
  waiting for transfers between devices  147 us (47%)
  starting transfers between devices  62.5 us (20%)
  blocking collectives  39.8 us (13%)
  local copies, waits for them, and re-layouts  22.8 us (7%)
  matrix products  16 us (5%)
  between operations  15.4 us (5%)
  other arithmetic  9.69 us (3%)
    ppermute x1, waiting for transfers between devices, on_device(): across = lax.ppermute(shard, 'section', SWAP)  46.9 us
    all_to_all x1, waiting for transfers between devices, on_device(): lax.all_to_all(result.reshape(groups, capacity, slice_width), GROUP, spli...  41.8 us
    all_to_all x2, waiting for transfers between devices, gather_rows(): lax.all_to_all(copies, axes, split_axis=0, concat_axis=0, tiled=True)  33.8 us
    all_gather x1, blocking collectives, on_device(): own = lax.all_gather(both, 'z', axis=0)  25.1 us
    all_to_all x1, waiting for transfers between devices, compact(): lax.all_to_all(copies.reshape(parts, slice_width, room), TENSOR, split_ax...  24.2 us
    all_to_all x1, starting transfers between devices, on_device(): lax.all_to_all(outgoing, GROUP, split_axis=0, concat_axis=0, tiled=True)  19.6 us
    all_to_all x1, blocking collectives, on_device(): lax.all_to_all(partial_out.transpose(3, 1, 0, 2, 4, 5).reshape(parts, -1,...  14.7 us
    all_to_all x1, starting transfers between devices, on_device(): lax.all_to_all(result.reshape(groups, capacity, slice_width), GROUP, spli...  12.6 us
  transfers between devices with their start and end apart: 10, of which 6 were waited for; matrix products, arithmetic and copies ran while one was open for 11% of the time, Pallas kernels for 0%

profile of v3, /device:TPU:1, one launch (start us, length us, event | category | flops | bytes accessed | tf_op | source)
XLA Modules:
  0.0 314.0 jit_solution(8417730903783267492)
XLA Ops:
  7.2 0.8 select_reduce_fusion.2
  9.0 1.2 convolution_convert_fusion.4
  10.8 1.0 pad_maximum_fusion.3
  11.8 19.6 %all-to-all-start.4 = ((bf16[64,16,364]{2,1,0:T(8,128)(2,1)}), bf16[64,16,364]{2,1,0:T(8,128)(2,1)S(1)}, u32[]{:S(2)}, u32[]{:S(2)}) async-start(bf16[64,16,364]{2,1,0:T(8,128)(2,1)} %pad_maximum_fusion.3), calls=%async_computation.4 | async-start | bytes 1572864 | tf_op jit(solution)/shard_map/all_to_all | solution.py:99
  31.5 2.2 collective-permute-start.1
  33.9 5.5 %collective-permute-start = (bf16[48,640]{1,0:T(8,128)(2,1)S(1)}, bf16[48,640]{1,0:T(8,128)(2,1)S(1)}, u32[]{:S(2)}, u32[]{:S(2)}) collective-permute-start(bf16[48,640]{1,0:T(8,128)(2,1)S(1)} %fusion.80), channel_id=1, source_target_pairs={{0,256},{256,0},{1,257},{257,1},{2,258},{258,2},{3,259},{259,3},{4... | collective-permute-start | bytes 184328 | tf_op jit(solution)/shard_map/ppermute | solution.py:77
  39.4 1.4 reshape_squeeze.3
  40.9 1.1 rev.16
  42.1 1.8 copy.118
  43.9 1.5 pad.25.clone
  45.4 46.9 %collective-permute-done = bf16[48,640]{1,0:T(8,128)(2,1)S(1)} collective-permute-done((bf16[48,640]{1,0:T(8,128)(2,1)S(1)}, bf16[48,640]{1,0:T(8,128)(2,1)S(1)}, u32[]{:S(2)}, u32[]{:S(2)}) %collective-permute-start) | collective-permute-done | bytes 61472 | tf_op jit(solution)/shard_map/ppermute | solution.py:77
  92.2 0.7 maximum_select_fusion
  92.9 1.0 fusion.60
  93.9 0.7 reduce_max.18
  95.3 77.4 %conditional.2 = (bf16[1024,360]{0,1:T(8,128)(2,1)S(1)}) conditional(s32[]{:T(128)} %convert_element_type.177, (bf16[1024,360]{1,0:T(8,128)(2,1)S(1)}, bf16[368,2880]{1,0:T(8,128)(2,1)}, bf16[8,184,360]{2,1,0:T(8,128)(2,1)S(1)}) %tuple.43, (s32[64]{0:T(128)S(1)}, s32[64,64]{1,0:T(8,128)S(1)}, s32[64,64]{1,0:T(8,128)S(1)}, f32[64]{0:T(128)S(1)}, ...), branch_computations={%region_7.8_spmd, %region_8.10_spmd} | conditional | flops 3579272960 | bytes 75708736
  97.4 0.6 fusion.14
  98.1 1.6 broadcast_in_dim.95
  99.7 4.2 %all-to-all-start.2 = ((bf16[8,360,384]{2,1,0:T(8,128)(2,1)}), bf16[8,360,384]{2,1,0:T(8,128)(2,1)S(1)}, u32[]{:S(2)}, u32[]{:S(2)}) async-start(bf16[8,360,384]{2,1,0:T(8,128)(2,1)} %bitcast.7), calls=%async_computation.2 | async-start | bytes 4423680 | tf_op jit(solution)/shard_map/cond/branch_1_fun/all_to_all | solution.py:174
  103.9 1.8 copy.120
  105.7 1.5 pad.18
  107.2 24.2 %all-to-all-done.2 = bf16[8,360,384]{2,1,0:T(8,128)(2,1)S(1)} async-done(((bf16[8,360,384]{2,1,0:T(8,128)(2,1)}), bf16[8,360,384]{2,1,0:T(8,128)(2,1)S(1)}, u32[]{:S(2)}, u32[]{:S(2)}) %all-to-all-start.2) | async-done | bytes 2211872 | tf_op jit(solution)/shard_map/cond/branch_1_fun/all_to_all | solution.py:174
  131.5 3.1 fusion.117
  134.6 1.3 convolution_bitcast_fusion.1
  136.1 1.6 broadcast_in_dim.110
  137.8 3.6 %all-to-all-start.3 = ((bf16[8,368,384]{2,1,0:T(8,128)(2,1)}), bf16[8,368,384]{2,1,0:T(8,128)(2,1)S(1)}, u32[]{:S(2)}, u32[]{:S(2)}) async-start(bf16[8,368,384]{2,1,0:T(8,128)(2,1)} %broadcast_in_dim.110), calls=%async_computation.3 | async-start | bytes 4521984 | tf_op jit(solution)/shard_map/cond/branch_1_fun/all_to_all | solution.py:18
  141.4 2.4 copy.99
  143.8 1.1 copy.98
  144.9 24.4 %all-to-all-done.3 = bf16[8,368,384]{2,1,0:T(8,128)(2,1)S(1)} async-done(((bf16[8,368,384]{2,1,0:T(8,128)(2,1)}), bf16[8,368,384]{2,1,0:T(8,128)(2,1)S(1)}, u32[]{:S(2)}, u32[]{:S(2)}) %all-to-all-start.3) | async-done | bytes 2261024 | tf_op jit(solution)/shard_map/cond/branch_1_fun/all_to_all | solution.py:18
  169.5 0.8 convolution_convert_fusion
  170.8 0.8 convolution_convert_fusion.1
  171.6 0.9 fusion.17
  172.8 1.2 copy.100
  173.9 12.6 %all-to-all-start.5 = ((bf16[64,16,360]{2,1,0:T(8,128)(2,1)}), bf16[64,16,360]{2,1,0:T(8,128)(2,1)S(1)}, u32[]{:S(2)}, u32[]{:S(2)}) async-start(bf16[64,16,360]{2,1,0:T(8,128)(2,1)} %bitcast.24), calls=%async_computation.5 | async-start | bytes 1572864 | tf_op jit(solution)/shard_map/all_to_all | solution.py:188
  186.9 41.8 %all-to-all-done.5 = bf16[64,16,360]{2,1,0:T(8,128)(2,1)S(1)} async-done(((bf16[64,16,360]{2,1,0:T(8,128)(2,1)}), bf16[64,16,360]{2,1,0:T(8,128)(2,1)S(1)}, u32[]{:S(2)}, u32[]{:S(2)}) %all-to-all-start.5) | async-done | bytes 737312 | tf_op jit(solution)/shard_map/all_to_all | solution.py:188
  230.0 1.0 broadcast_in_dim.175
  231.0 3.5 %all-to-all-start.6 = ((bf16[8,384,128]{2,1,0:T(8,128)(2,1)}), bf16[8,384,128]{2,1,0:T(8,128)(2,1)S(1)}, u32[]{:S(2)}, u32[]{:S(2)}) async-start(bf16[8,384,128]{2,1,0:T(8,128)(2,1)} %broadcast_in_dim.175), calls=%async_computation.6 | async-start | bytes 1572864 | tf_op jit(solution)/shard_map/all_to_all | solution.py:18
  234.5 1.9 collective-permute-start.2
  236.9 9.5 %all-to-all-done.6 = bf16[8,384,128]{2,1,0:T(8,128)(2,1)S(1)} async-done(((bf16[8,384,128]{2,1,0:T(8,128)(2,1)}), bf16[8,384,128]{2,1,0:T(8,128)(2,1)S(1)}, u32[]{:S(2)}, u32[]{:S(2)}) %all-to-all-start.6) | async-done | bytes 786464 | tf_op jit(solution)/shard_map/all_to_all | solution.py:18
  247.4 0.9 copy-done.6
  249.5 25.1 %all_gather.7 = bf16[16,128,128]{2,1,0:T(8,128)(2,1)S(1)} all-gather(bf16[1,128,128]{2,1,0:T(8,128)(2,1)S(1)} %bitcast.163), channel_id=1, replica_groups=mesh['section'=2,'z'=16,'core'=2,'xlo'=2,'y'=4] {'z'}, dimensions={0}, use_global_device_ids=true | all-gather | bytes 557056 | tf_op jit(solution)/shard_map/all_gather | solution.py:227
  274.7 9.3 %collective-permute-start.3 = (bf16[16,128,128]{2,1,0:T(8,128)(2,1)S(1)}, bf16[16,128,128]{2,1,0:T(8,128)(2,1)S(1)}, u32[]{:S(2)}, u32[]{:S(2)}) collective-permute-start(bf16[16,128,128]{2,1,0:T(8,128)(2,1)S(1)} %all_gather.7), channel_id=1, source_target_pairs={{0,8},{8,0},{1,9},{9,1},{2,10},{10,2},{3,11},{11,3},{4,12},{12,4},... | collective-permute-start | bytes 1572872 | tf_op jit(solution)/shard_map/ppermute | solution.py:228
  284.0 0.7 broadcast_compare_fusion.1
  284.8 0.7 collective-permute-done.3
  285.6 1.3 fusion.26
  286.9 1.8 fusion.27
  288.7 1.9 fusion.54
  291.6 14.7 %all_to_all.38 = bf16[8,384,128]{2,1,0:T(8,128)(2,1)S(1)} all-to-all(bf16[8,384,128]{2,1,0:T(8,128)(2,1)S(1)} %bitcast.139), channel_id=1, replica_groups=mesh['section'=2,'z'=16,'core'=2,'xlo'=2,'y'=4] {'xlo','y'}, dimensions={0} | all-to-all | bytes 1572864 | tf_op jit(solution)/shard_map/all_to_all | solution.py:259
  306.4 0.7 reshape.626
  (123 shorter events, 10.2 us)
Async XLA Ops:
  7.2 1.8 copy-start.7
  8.0 0.6 copy-start.11
  10.6 23.1 %copy-start.9 = (bf16[256,45]{0,1:T(8,128)(2,1)S(1)}, bf16[256,45]{0,1:T(8,128)(2,1)}, u32[]{:S(2)}) copy-start(bf16[256,45]{0,1:T(8,128)(2,1)} %param.23) | copy-start | bytes 69124
  10.6 23.1 %copy-start.10 = (bf16[45,256]{1,0:T(8,128)(2,1)S(1)}, bf16[45,256]{1,0:T(8,128)(2,1)}, u32[]{:S(2)}) copy-start(bf16[45,256]{1,0:T(8,128)(2,1)} %param.20) | copy-start | bytes 69124
  10.6 23.1 %copy-start.13 = (bf16[45,64]{1,0:T(8,128)(2,1)S(1)}, bf16[45,64]{1,0:T(8,128)(2,1)}, u32[]{:S(2)}) copy-start(bf16[45,64]{1,0:T(8,128)(2,1)} %param.22) | copy-start | bytes 17284
  10.7 23.1 %copy-start.14 = (bf16[45,64]{1,0:T(8,128)(2,1)S(1)}, bf16[45,64]{1,0:T(8,128)(2,1)}, u32[]{:S(2)}) copy-start(bf16[45,64]{1,0:T(8,128)(2,1)} %param.21) | copy-start | bytes 17284
  11.8 81.1 %all-to-all-start.4 = ((bf16[64,16,364]{2,1,0:T(8,128)(2,1)}), bf16[64,16,364]{2,1,0:T(8,128)(2,1)S(1)}, u32[]{:S(2)}, u32[]{:S(2)}) async-start(bf16[64,16,364]{2,1,0:T(8,128)(2,1)} %pad_maximum_fusion.3), calls=%async_computation.4 | async-start | bytes 1572864 | tf_op jit(solution)/shard_map/all_to_all | solution.py:99
  31.5 203.1 %all-gather.2.cloned.1.call-start = ((), (), s32[]{:S(2)}) async-start(), calls=%async_computation.8 | async-start | bytes 2088960 | tf_op jit(solution)/shard_map/all_gather | solution.py:101
  31.5 63.8 %collective-permute-start.1 = (bf16[1,2,180,2880]{3,1,2,0:T(2,128)(2,1)}, bf16[1,2,180,2880]{3,1,2,0:T(2,128)(2,1)}, u32[]{:S(2)}, u32[]{:S(2)}) collective-permute-start(bf16[1,2,180,2880]{3,1,2,0:T(2,128)(2,1)} %param.17), channel_id=1, source_target_pairs={{0,4},{4,0},{1,5},{5,1},{2,6},{6,2},{3,7},{7,3},{8,12},{12,8},{9,1... | collective-permute-start | bytes 6220808 | tf_op jit(solution)/shard_map/ppermute | solution.py:73
  33.9 58.4 %collective-permute-start = (bf16[48,640]{1,0:T(8,128)(2,1)S(1)}, bf16[48,640]{1,0:T(8,128)(2,1)S(1)}, u32[]{:S(2)}, u32[]{:S(2)}) collective-permute-start(bf16[48,640]{1,0:T(8,128)(2,1)S(1)} %fusion.80), channel_id=1, source_target_pairs={{0,256},{256,0},{1,257},{257,1},{2,258},{258,2},{3,259},{259,3},{4... | collective-permute-start | bytes 184328 | tf_op jit(solution)/shard_map/ppermute | solution.py:77
  99.7 31.7 %all-to-all-start.2 = ((bf16[8,360,384]{2,1,0:T(8,128)(2,1)}), bf16[8,360,384]{2,1,0:T(8,128)(2,1)S(1)}, u32[]{:S(2)}, u32[]{:S(2)}) async-start(bf16[8,360,384]{2,1,0:T(8,128)(2,1)} %bitcast.7), calls=%async_computation.2 | async-start | bytes 4423680 | tf_op jit(solution)/shard_map/cond/branch_1_fun/all_to_all | solution.py:174
  131.5 3.1 copy-start.1
  137.8 31.5 %all-to-all-start.3 = ((bf16[8,368,384]{2,1,0:T(8,128)(2,1)}), bf16[8,368,384]{2,1,0:T(8,128)(2,1)S(1)}, u32[]{:S(2)}, u32[]{:S(2)}) async-start(bf16[8,368,384]{2,1,0:T(8,128)(2,1)} %broadcast_in_dim.110), calls=%async_computation.3 | async-start | bytes 4521984 | tf_op jit(solution)/shard_map/cond/branch_1_fun/all_to_all | solution.py:18
  144.9 24.6 %copy-start.3 = (bf16[4,2,184,360]{3,2,1,0:T(8,128)(2,1)S(1)}, bf16[4,2,184,360]{3,2,1,0:T(8,128)(2,1)}, u32[]{:S(2)}) copy-start(bf16[4,2,184,360]{3,2,1,0:T(8,128)(2,1)} %copy.99) | copy-start | bytes 3179524 | tf_op jit(solution)/shard_map/conditional
  169.5 1.3 copy-start.2
  172.7 13.8 %copy-start.15 = (f32[2880]{0:T(1024)S(1)}, f32[2880]{0:T(1024)}, u32[]{:S(2)}) copy-start(f32[2880]{0:T(1024)} %param.19) | copy-start | bytes 34564
  172.7 14.1 %copy-start.12 = (s32[128,4]{0,1:T(4,128)S(1)}, s32[128,4]{0,1:T(4,128)}, u32[]{:S(2)}) copy-start(s32[128,4]{0,1:T(4,128)} %copy-done.11) | copy-start | bytes 6148
  172.7 14.1 %copy-start.16 = (f32[128,4]{0,1:T(4,128)S(1)}, f32[128,4]{0,1:T(4,128)}, u32[]{:S(2)}) copy-start(f32[128,4]{0,1:T(4,128)} %param.15) | copy-start | bytes 6148
  172.8 55.9 %copy-start.8 = (s32[1024]{0:T(1024)S(1)}, s32[1024]{0:T(1024)}, u32[]{:S(2)}) copy-start(s32[1024]{0:T(1024)} %copy-done.7) | copy-start | bytes 12292
  172.8 56.5 %copy-start.4 = (bf16[128,360]{0,1:T(8,128)(2,1)S(1)}, bf16[128,360]{0,1:T(8,128)(2,1)}, u32[]{:S(2)}) copy-start(bf16[128,360]{0,1:T(8,128)(2,1)} %param.13) | copy-start | bytes 276484
  173.9 54.7 %all-to-all-start.5 = ((bf16[64,16,360]{2,1,0:T(8,128)(2,1)}), bf16[64,16,360]{2,1,0:T(8,128)(2,1)S(1)}, u32[]{:S(2)}, u32[]{:S(2)}) async-start(bf16[64,16,360]{2,1,0:T(8,128)(2,1)} %bitcast.24), calls=%async_computation.5 | async-start | bytes 1572864 | tf_op jit(solution)/shard_map/all_to_all | solution.py:188
  229.8 17.4 %copy-start.5 = (bf16[128,360]{0,1:T(8,128)(2,1)}, bf16[128,360]{0,1:T(8,128)(2,1)S(1)}, u32[]{:S(2)}) copy-start(bf16[128,360]{0,1:T(8,128)(2,1)S(1)} %fusion.45) | copy-start | bytes 276484
  231.0 15.4 %all-to-all-start.6 = ((bf16[8,384,128]{2,1,0:T(8,128)(2,1)}), bf16[8,384,128]{2,1,0:T(8,128)(2,1)S(1)}, u32[]{:S(2)}, u32[]{:S(2)}) async-start(bf16[8,384,128]{2,1,0:T(8,128)(2,1)} %broadcast_in_dim.175), calls=%async_computation.6 | async-start | bytes 1572864 | tf_op jit(solution)/shard_map/all_to_all | solution.py:18
  234.5 14.3 %collective-permute-start.2 = (bf16[1536,640]{1,0:T(8,128)(2,1)}, bf16[1536,640]{1,0:T(8,128)(2,1)S(1)}, u32[]{:S(2)}, u32[]{:S(2)}) collective-permute-start(bf16[1536,640]{1,0:T(8,128)(2,1)} %all-gather.2.cloned.1.call-done), channel_id=1, source_target_pairs={{0,8},{8,0},{1,9},{9,1},{2,10},{10,2},{3,11},{11,3},{4,12},{12,4},... | collective-permute-start | bytes 5898248 | tf_op jit(solution)/shard_map/ppermute | solution.py:187
  246.8 1.6 copy-start.6
  274.7 10.8 %collective-permute-start.3 = (bf16[16,128,128]{2,1,0:T(8,128)(2,1)S(1)}, bf16[16,128,128]{2,1,0:T(8,128)(2,1)S(1)}, u32[]{:S(2)}, u32[]{:S(2)}) collective-permute-start(bf16[16,128,128]{2,1,0:T(8,128)(2,1)S(1)} %all_gather.7), channel_id=1, source_target_pairs={{0,8},{8,0},{1,9},{9,1},{2,10},{10,2},{3,11},{11,3},{4,12},{12,4},... | collective-permute-start | bytes 1572872 | tf_op jit(solution)/shard_map/ppermute | solution.py:228
Sparse Core Ops, SparseCore 0:
  93.1 61.8 all-gather.1
